TPU v7x, 256 devices: a whole 4x4x8 slice. The times are simulated.
256 devices in a mesh: gx: 32 (over z_lo, x, core), gz: 8 (over y, z_hi).
Axes of the slice: x: 4, y: 4, z: 8 (z_hi: 2, z_lo: 4; z = z_hi * 4 + z_lo), core: 2. Of those that a mesh axis runs over, the one named last changes fastest.
Arguments:
- u_vel: bfloat16 [512, 384, 768], P('gx', 'gz'), may hold values from -6 to 6
- v_vel: bfloat16 [512, 384, 768], P('gx', 'gz'), may hold values from -6 to 6
- w_vel: bfloat16 [512, 384, 768], P('gx', 'gz'), may hold values from -6 to 6
Outputs:
- pressure: float32 [512, 384, 768], P('gx', 'gz')
- u_new: float32 [512, 384, 768], P('gx', 'gz')
- v_new: float32 [512, 384, 768], P('gx', 'gz')
- w_new: float32 [512, 384, 768], P('gx', 'gz')
All inputs are finite; a program needn't handle non-finite values.
Results may differ from a plain program's by a relative error of at most 0.002.
Values may be sent and summed in bfloat16 or wider, within the bound.
A program may use at most 128 MiB of HBM per device.

v0:
```python
import functools
import math

import jax
import jax.numpy as jnp
import numpy as np
from jax import lax
from jax.experimental import pallas as pl
from jax.experimental.pallas import tpu as pltpu
from jax.sharding import PartitionSpec as P

F32 = jnp.float32
BF16 = jnp.bfloat16
TILE = 256
LANES = 128


def hartley_np(count):
    index = np.arange(count)
    angle = (index[:, None] * index[None, :] % count) * (2.0 * np.pi / count)
    return np.cos(angle) + np.sin(angle)


def sine_np(count):
    index = np.arange(1, count + 1)
    angle = (index[:, None] * index[None, :] % (2 * (count + 1))) * (np.pi / (count + 1))
    return np.sqrt(2.0 / (count + 1)) * np.sin(angle)


def sine_parts_np(count, step):
    mode = np.arange(1, count + 1)
    coarse = np.arange(0, count, step)
    fine = np.arange(1, step + 1)
    size = np.sqrt(2.0 / (count + 1))
    angle_c = (coarse[:, None] * mode % (2 * (count + 1))) * (np.pi / (count + 1))
    angle_f = (fine[:, None] * mode % (2 * (count + 1))) * (np.pi / (count + 1))
    return (
        size * np.sin(angle_c),
        size * np.cos(angle_c),
        np.sin(angle_f),
        np.cos(angle_f),
    )


def wall_eigen_np(count):
    return 4.0 * np.sin(np.arange(1, count + 1) * (np.pi / (2 * count + 2))) ** 2


def periodic_eigen_np(count):
    return 4.0 * np.sin(np.arange(count) * (np.pi / count)) ** 2


def edge_rows(cx, cz):
    grid = np.arange(cx * cz).reshape(cx, cz)
    return np.concatenate([grid[0], grid[-1], grid[:, 0], grid[:, -1]])


def f32(array):
    return np.ascontiguousarray(np.asarray(array, np.float32))


def halves(array):
    array = np.asarray(array, np.float32)
    high = array.astype(BF16)
    low = (array - high.astype(np.float32)).astype(BF16)
    return [high, low]


def split(x):
    high = x.astype(BF16)
    return high, (x - high.astype(F32)).astype(BF16)


def dot(a, b):
    return jnp.dot(a, b, preferred_element_type=F32)


def dot_t(a, b):
    return lax.dot_general(a, b, (((1,), (1,)), ((), ())), preferred_element_type=F32)


def dot3(a, b, op=dot):
    return op(a[0], b[0]) + op(a[1], b[0]) + op(a[0], b[1])


def fill_sine(parts, high, low):
    sa, ca, sb, cb = parts
    step = sb.shape[0]

    @pl.loop(0, sa.shape[0])
    def _(a):
        block = sa[pl.ds(a, 1), :] * cb[...] + ca[pl.ds(a, 1), :] * sb[...]
        rows = pl.ds(pl.multiple_of(a * step, step), step)
        high[rows, :], low[rows, :] = split(block)


def fill_local(sx, sz, high, low):
    step = sz.shape[0]

    @pl.loop(0, sx.shape[0])
    def _(a):
        rows = pl.ds(pl.multiple_of(a * step, step), step)
        high[rows, :], low[rows, :] = split(sx[pl.ds(a, 1), :] * sz[...])


def along_rows(x, first, last):
    rows = x.shape[0]
    at = lax.broadcasted_iota(jnp.int32, x.shape, 0)
    up = jnp.where(at == rows - 1, last, pltpu.roll(x, rows - 1, 0))
    down = jnp.where(at == 0, first, pltpu.roll(x, 1, 0))
    return up - down


def along_lanes(x):
    lanes = x.shape[1]
    at = lax.broadcasted_iota(jnp.int32, x.shape, 1)
    up = jnp.where(at == lanes - 1, 0.0, pltpu.roll(x, lanes - 1, 1))
    down = jnp.where(at == 0, 0.0, pltpu.roll(x, 1, 1))
    return up - down


def forward_kernel(
    u, v, w, sa, ca, sb, cb, sx, sz, eh, el, mux, mum, send, modes, sh, sl, kh, kl, dh, dl
):
    cx, cz, ny = u.shape
    cells = cx * cz
    fill_sine((sa, ca, sb, cb), sh, sl)
    fill_local(sx, sz, kh, kl)

    @pl.loop(0, cx)
    def _(x):
        after = u[jnp.minimum(x + 1, cx - 1)].astype(F32) * jnp.where(x < cx - 1, 1.0, 0.0)
        before = u[jnp.maximum(x - 1, 0)].astype(F32) * jnp.where(x > 0, 1.0, 0.0)
        div = 0.5 * (
            (after - before)
            + along_lanes(v[x].astype(F32))
            + along_rows(w[x].astype(F32), 0.0, 0.0)
        )
        rows = pl.ds(pl.multiple_of(x * cz, cz), cz)
        dh[rows, :], dl[rows, :] = split(div)

    dh[cells : cells + cz, :] = (-0.5 * u[0].astype(F32)).astype(BF16)
    dh[cells + cz : cells + 2 * cz, :] = (0.5 * u[cx - 1].astype(F32)).astype(BF16)
    dh[cells + 2 * cz : cells + 2 * cz + cx, :] = (-0.5 * w[:, 0, :].astype(F32)).astype(BF16)
    dh[cells + 2 * cz + cx :, :] = (0.5 * w[:, cz - 1, :].astype(F32)).astype(BF16)

    @pl.loop(0, ny // TILE)
    def _(n):
        cols = pl.ds(pl.multiple_of(n * TILE, TILE), TILE)
        wide = dot(dh[...], sh[:, cols]) + dot(dh[...], sl[:, cols])
        field = wide[:cells] + dot(dl[...], sh[:, cols])
        mode = dot3((kh[...], kl[...]), split(field))
        modes[:, cols] = mode
        mode = mode / (mux[...] + mum[:, cols])
        edge = wide[cells:] - dot3((eh[...], el[...]), split(mode))
        send[cols, :] = edge.T


def owner_kernel(
    ngx, ngz, cx, cz, seen, hxh, hxl, hzh, hzl, lxh, lxl, lxth, lxtl, lzth, lztl, muz, mukx, mum, out
):
    per = mum.shape[0]
    nx, nz = ngx * cx, ngz * cz
    lane = lax.broadcasted_iota(jnp.int32, (ngx, LANES), 1)
    lane8 = lax.broadcasted_iota(jnp.int32, (ngz, LANES), 1)
    wide_x = nz // LANES
    wide_z = nx // LANES
    hx = (hxh[...], hxl[...])
    hz = (hzh[...], hzl[...])
    px, pz = [], []
    for m in range(per):
        cols = [[jnp.zeros((ngx, LANES), F32)] * wide_x for _ in range(2)]
        for j in range(ngz):
            piece = seen[pl.ds(j * per + m, ngx, stride=ngz * per), :]
            for f in range(2):
                turned = pltpu.roll(piece, (cz * j - cz * f) % LANES, 1)
                for c in range(wide_x):
                    low, high = cz * j - c * LANES, cz * (j + 1) - c * LANES
                    if high > 0 and low < LANES:
                        cols[f][c] = jnp.where((lane >= low) & (lane < high), turned, cols[f][c])
        px += [jnp.concatenate(c, 1) for c in cols]
        cols = [[jnp.zeros((ngz, LANES), F32)] * wide_z for _ in range(2)]
        for i in range(ngx):
            piece = seen[pl.ds(i * ngz * per + m, ngz, stride=per), :]
            c, low = cx * i // LANES, cx * i % LANES
            for f in range(2):
                turned = pltpu.roll(piece, (low - 2 * cz - cx * f) % LANES, 1)
                cols[f][c] = jnp.where((lane8 >= low) & (lane8 < low + cx), turned, cols[f][c])
        pz += [jnp.concatenate(c, 1) for c in cols]
    f1 = dot3(split(jnp.concatenate(px, 0)), hz)
    f2 = dot3(split(jnp.concatenate(pz, 0)), hx)
    ex, ez = [], []
    for m in range(per):
        mine = f1[2 * ngx * m : 2 * ngx * (m + 1)]
        other = f2[2 * ngz * m : 2 * ngz * (m + 1)].T
        spec = dot3((lxh[...], lxl[...]), split(mine)) + dot3(split(other), (lzth[...], lztl[...]))
        spec = spec / ((mukx[...] + muz[...] + mum[m : m + 1, :1]) * (-float(nx * nz)))
        spec = split(spec)
        ex.append(dot3((lxth[...], lxtl[...]), spec))
        ez.append(dot3((lzth[...], lztl[...]), spec, dot_t))
    ex = -dot3(split(jnp.concatenate(ex, 0)), hz)
    ez = -dot3(split(jnp.concatenate(ez, 0)), hx)
    for m in range(per):
        tx, tz = [], []
        for f in range(2):
            at = 2 * ngx * m + f * ngx
            turn = 1 if f == 0 else ngx - 1
            tx.append(ex[at : at + ngx] + pltpu.roll(px[2 * m + 1 - f], turn, 0))
            at = 2 * ngz * m + f * ngz
            turn = 1 if f == 0 else ngz - 1
            tz.append(ez[at : at + ngz] + pltpu.roll(pz[2 * m + 1 - f], turn, 0))
        for j in range(ngz):
            c, low = cz * j // LANES, cz * j % LANES
            total = jnp.zeros((ngx, LANES), F32)
            for f in range(2):
                piece = tx[f][:, c * LANES : (c + 1) * LANES]
                if low + cz > LANES:
                    after = tx[f][:, (c + 1) * LANES : (c + 2) * LANES]
                    piece = jnp.where(lane >= low, piece, after)
                piece = pltpu.roll(piece, (cz * f - low) % LANES, 1)
                total = jnp.where((lane >= cz * f) & (lane < cz * (f + 1)), piece, total)
            out[pl.ds(j * per + m, ngx, stride=ngz * per), :] = total
        for i in range(ngx):
            c, low = cx * i // LANES, cx * i % LANES
            rows = pl.ds(i * ngz * per + m, ngz, stride=per)
            total = out[rows, :]
            for f in range(2):
                start = 2 * cz + cx * f
                piece = pltpu.roll(tz[f][:, c * LANES : (c + 1) * LANES], (start - low) % LANES, 1)
                total = jnp.where((lane8 >= start) & (lane8 < start + cx), piece, total)
            out[rows, :] = total


def backward_kernel(
    u, v, w, ul, uh, wl, wh, got, modes, sa, ca, sb, cb, sx, sz, eth, etl, mux, mum,
    pressure, u_new, v_new, w_new, sh, sl, kh, kl, fh, fl, ring, plow, phigh,
):
    cx, cz, ny = u.shape
    cells = cx * cz
    fill_sine((sa, ca, sb, cb), sh, sl)
    fill_local(sx, sz, kh, kl)

    @pl.loop(0, ny // TILE)
    def _(n):
        cols = pl.ds(pl.multiple_of(n * TILE, TILE), TILE)
        edge = split(got[cols, :].T)
        field = dot3((eth[...], etl[...]), edge) - modes[:, cols]
        field = split(field / (mux[...] + mum[:, cols]))
        field = split(dot3((kh[...], kl[...]), field))
        fh[:cells, cols], fl[:cells, cols] = field
        fh[cells:, cols], fl[cells:, cols] = edge

    @pl.loop(0, ny // TILE)
    def _(n):
        cols = pl.ds(pl.multiple_of(n * TILE, TILE), TILE)
        wide = dot3((fh[...], fl[...]), (sh[:, cols], sl[:, cols]))
        pressure[:, :, cols] = wide[:cells].reshape(cx, cz, TILE)
        ring[:, cols] = wide[cells:]

    plow[...] = ring[:cz, :] - 0.5 * ul[...].astype(F32)
    phigh[...] = ring[cz : 2 * cz, :] + 0.5 * uh[...].astype(F32)
    edge = pl.ds(2 * cz, cx)
    ring[edge, :] = ring[edge, :] - 0.5 * wl[...].astype(F32)
    edge = pl.ds(2 * cz + cx, cx)
    ring[edge, :] = ring[edge, :] + 0.5 * wh[...].astype(F32)

    def finish(x, before, after):
        here = pressure[x]
        u_new[x] = u[x].astype(F32) - 0.5 * (after - before)
        v_new[x] = v[x].astype(F32) - 0.5 * along_lanes(here)
        first = ring[pl.ds(2 * cz + x, 1), :]
        last = ring[pl.ds(2 * cz + cx + x, 1), :]
        w_new[x] = w[x].astype(F32) - 0.5 * along_rows(here, first, last)

    finish(0, plow[...], pressure[1])
    finish(cx - 1, pressure[cx - 2], phigh[...])

    @pl.loop(1, cx - 1)
    def _(x):
        finish(x, pressure[x - 1], pressure[x + 1])


def shifted(block, axis, step):
    count = lax.axis_size(axis)
    return lax.ppermute(block, axis, [(i, (i + step) % count) for i in range(count)])


def call(kernel, name, outs, scratch, flops, *args):
    size = sum(math.prod(a.shape) * a.dtype.itemsize for a in [*args, *outs])
    return pl.pallas_call(
        kernel,
        out_shape=outs,
        in_specs=[pl.BlockSpec(memory_space=pltpu.VMEM)] * len(args),
        out_specs=[pl.BlockSpec(memory_space=pltpu.VMEM)] * len(outs),
        scratch_shapes=scratch,
        compiler_params=pltpu.CompilerParams(vmem_limit_bytes=60 << 20),
        cost_estimate=pl.CostEstimate(flops=flops, bytes_accessed=size, transcendentals=0),
        name=name,
    )(*args)


def on_device(u_vel, v_vel, w_vel):
    cx, cz, ny = u_vel.shape
    ngx = lax.axis_size("gx")
    ngz = lax.axis_size("gz")
    nx, nz = ngx * cx, ngz * cz
    devices = ngx * ngz
    per = ny // devices
    cells = cx * cz
    edges = 2 * (cx + cz)
    me = lax.axis_index("gx") * ngz + lax.axis_index("gz")
    u_low = shifted(u_vel[-1], "gx", 1)
    u_high = shifted(u_vel[0], "gx", -1)
    w_low = shifted(w_vel[:, -1], "gz", 1)
    w_high = shifted(w_vel[:, 0], "gz", -1)
    local = np.kron(sine_np(cx), sine_np(cz))[edge_rows(cx, cz)]
    tables = [f32(t) for t in sine_parts_np(ny, 32)]
    tables += [f32(np.repeat(sine_np(cx), cz, 1)), f32(np.tile(sine_np(cz), (1, cx)))]
    mux = f32(np.add.outer(wall_eigen_np(cx), wall_eigen_np(cz)).reshape(-1, 1))
    mum = f32(wall_eigen_np(ny).reshape(1, -1))
    shape = jax.ShapeDtypeStruct
    square = [pltpu.VMEM((ny, ny), BF16)] * 2 + [pltpu.VMEM((cells, cells), BF16)] * 2
    send, modes = call(
        forward_kernel,
        "forward",
        [shape((ny, edges), F32), shape((cells, ny), F32)],
        square + [pltpu.VMEM((cells + edges, ny), BF16), pltpu.VMEM((cells, ny), BF16)],
        6 * cells * ny * (ny + cells + edges),
        u_vel, v_vel, w_vel, *tables, *halves(local), mux, mum,
    )
    send = send.reshape(devices, per, 1, edges)
    seen = lax.all_to_all(send, ("gx", "gz"), split_axis=0, concat_axis=0, tiled=True)
    hx, hz = hartley_np(nx), hartley_np(nz)
    block_x, block_z = np.arange(ngx) * cx, np.arange(ngz) * cz
    lx = hx[:, np.concatenate([(block_x - 1) % nx, (block_x + cx) % nx])]
    lz = hz[:, np.concatenate([(block_z - 1) % nz, (block_z + cz) % nz])]
    lam_m = lax.dynamic_slice(jnp.asarray(mum[0]), (me * per,), (per,))
    (back,) = call(
        functools.partial(owner_kernel, ngx, ngz, cx, cz),
        "owner",
        [shape((ny, edges), F32)],
        [],
        6 * per * nx * nz * 200,
        seen.reshape(ny, edges),
        *halves(hx), *halves(hz), *halves(lx), *halves(lx.T), *halves(lz.T),
        f32(periodic_eigen_np(nz).reshape(1, -1)),
        f32(periodic_eigen_np(nx).reshape(-1, 1)),
        jnp.broadcast_to(lam_m[:, None], (per, LANES)),
    )
    back = back.reshape(devices, per, 1, edges)
    got = lax.all_to_all(back, ("gx", "gz"), split_axis=0, concat_axis=0, tiled=True)
    block = shape((cx, cz, ny), F32)
    return tuple(
        call(
            backward_kernel,
            "backward",
            [block] * 4,
            square
            + [pltpu.VMEM((cells + edges, ny), BF16)] * 2
            + [pltpu.VMEM((edges, ny), F32)]
            + [pltpu.VMEM((cz, ny), F32)] * 2,
            6 * cells * ny * (ny + cells + edges),
            u_vel, v_vel, w_vel, u_low, u_high, w_low, w_high, got.reshape(ny, edges), modes,
            *tables, *halves(local.T), mux, mum,
        )
    )


def solution(mesh):
    spec = P("gx", "gz", None)
    return jax.shard_map(
        on_device, mesh=mesh, in_specs=(spec,) * 3, out_specs=(spec,) * 4, check_vma=False
    )
```

profile of v0, /device:TPU:1, one launch (start us, length us, event | category | flops | bytes accessed | tf_op | source)
XLA Modules:
  0.0 110.3 jit_solution(606966230720941219)
XLA Ops:
  0.6 20.4 %forward.1 = (f32[768,128]{1,0:T(8,128)}, f32[768,768]{1,0:T(8,128)}) custom-call(bf16[16,48,768]{2,1,0:T(8,128)(2,1)} %u.3, bf16[16,48,768]{2,1,0:T(8,128)(2,1)} %v.3, bf16[16,48,768]{2,1,0:T(8,128)(2,1)} %w.3, f32[24,768]{1,0:T(8,128)} %constant.67.clone.sa, f32[24,768]{1,0:T(8,128)} %constant.68.clone.ca, f32[32,768]{1,0:T(8,128)} %constant.69.clone.sb, ...), custom_call_target="tpu_custom_call" | custom-call | flops 5888802816 | bytes 7231488 | tf_op jit(solution)/shard_map/forward/pallas_call | solution.py:290
  21.0 15.7 %all-to-all-start = ((f32[256,3,1,128]{3,2,1,0:T(1,128)}), f32[256,3,1,128]{3,2,1,0:T(1,128)S(1)}, u32[]{:S(2)}, u32[]{:S(2)}) async-start(f32[256,3,1,128]{3,2,1,0:T(1,128)} %bitcast.17), calls=%async_computation | async-start | bytes 786432 | tf_op jit(solution)/shard_map/all_to_all | solution.py:332
  36.7 0.8 dynamic_slice.3
  37.4 17.7 %all-to-all-done = f32[256,3,1,128]{3,2,1,0:T(1,128)S(1)} async-done(((f32[256,3,1,128]{3,2,1,0:T(1,128)}), f32[256,3,1,128]{3,2,1,0:T(1,128)S(1)}, u32[]{:S(2)}, u32[]{:S(2)}) %all-to-all-start) | async-done | bytes 393248 | tf_op jit(solution)/shard_map/all_to_all | solution.py:332
  55.2 0.0 copy-start
  55.2 0.7 broadcast_in_dim.2.mum
  55.9 0.0 copy-done
  55.9 9.1 %owner.1 = f32[768,128]{1,0:T(8,128)} custom-call(f32[768,128]{1,0:T(8,128)} %bitcast.15, bf16[512,512]{1,0:T(8,128)(2,1)} %constant.78.clone.hxh, bf16[512,512]{1,0:T(8,128)(2,1)} %constant.79.clone.hxl, bf16[384,384]{1,0:T(8,128)(2,1)} %constant.80.clone.hzh, bf16[384,384]{1,0:T(8,128)(2,1)} %constant.81.clone.hzl, bf16[512,64]{1,0:T(8,128)(2,1)} %constant.82.clone.lxh, ...), custom_call_target="tpu_custom_call" | custom-call | flops 707788800 | bytes 2716672 | tf_op jit(solution)/shard_map/owner/pallas_call | solution.py:290
  65.1 5.4 %all-to-all-start.1 = ((f32[256,3,1,128]{3,2,1,0:T(1,128)}), f32[256,3,1,128]{3,2,1,0:T(1,128)S(1)}, u32[]{:S(2)}, u32[]{:S(2)}) async-start(f32[256,3,1,128]{3,2,1,0:T(1,128)} %bitcast.14), calls=%async_computation.1 | async-start | bytes 786432 | tf_op jit(solution)/shard_map/all_to_all | solution.py:351
  70.5 0.9 slice_bitcast_fusion
  71.4 2.4 %collective-permute-start.1 = (bf16[48,768]{1,0:T(8,128)(2,1)S(1)}, bf16[48,768]{1,0:T(8,128)(2,1)S(1)}, u32[]{:S(2)}, u32[]{:S(2)}) collective-permute-start(bf16[48,768]{1,0:T(8,128)(2,1)S(1)} %get-tuple-element.10), channel_id=1, source_target_pairs={{0,248},{8,0},{16,8},{24,16},{32,24},{40,32},{48,40},{56,48},{64,5... | collective-permute-start | bytes 221192 | tf_op jit(solution)/shard_map/ppermute | solution.py:285
  73.8 0.0 collective-permute-start
  73.8 1.1 fusion
  74.9 5.9 %collective-permute-start.2 = (bf16[16,768]{1,0:T(8,128)(2,1)S(1)}, bf16[16,768]{1,0:T(8,128)(2,1)S(1)}, u32[]{:S(2)}, u32[]{:S(2)}) collective-permute-start(bf16[16,768]{1,0:T(8,128)(2,1)S(1)} %bitcast.18), channel_id=1, source_target_pairs={{0,1},{1,2},{2,3},{3,4},{4,5},{5,6},{6,7},{7,0},{8,9},{9,10},{10,1... | collective-permute-start | bytes 73736 | tf_op jit(solution)/shard_map/ppermute | solution.py:285
  80.8 2.6 %collective-permute-start.3 = (bf16[16,768]{1,0:T(8,128)(2,1)S(1)}, bf16[16,768]{1,0:T(8,128)(2,1)S(1)}, u32[]{:S(2)}, u32[]{:S(2)}) collective-permute-start(bf16[16,768]{1,0:T(8,128)(2,1)S(1)} %bitcast.19), channel_id=1, source_target_pairs={{0,7},{1,0},{2,1},{3,2},{4,3},{5,4},{6,5},{7,6},{8,15},{9,8},{10,9... | collective-permute-start | bytes 73736 | tf_op jit(solution)/shard_map/ppermute | solution.py:285
  83.4 3.8 %collective-permute-done.2.wl = bf16[16,768]{1,0:T(8,128)(2,1)S(1)} collective-permute-done((bf16[16,768]{1,0:T(8,128)(2,1)S(1)}, bf16[16,768]{1,0:T(8,128)(2,1)S(1)}, u32[]{:S(2)}, u32[]{:S(2)}) %collective-permute-start.2) | collective-permute-done | bytes 24608 | tf_op jit(solution)/shard_map/ppermute | solution.py:285
  87.2 0.0 copy-start.4
  87.2 0.6 collective-permute-done.3.wh
  87.8 0.0 copy-start.5
  87.8 0.0 collective-permute-done.1.uh
  87.8 0.0 copy-start.2
  87.8 0.0 collective-permute-done.ul
  87.8 0.0 copy-start.3
  87.8 1.3 %all-to-all-done.1 = f32[256,3,1,128]{3,2,1,0:T(1,128)S(1)} async-done(((f32[256,3,1,128]{3,2,1,0:T(1,128)}), f32[256,3,1,128]{3,2,1,0:T(1,128)S(1)}, u32[]{:S(2)}, u32[]{:S(2)}) %all-to-all-start.1) | async-done | bytes 393248 | tf_op jit(solution)/shard_map/all_to_all | solution.py:351
  89.1 0.0 copy-start.1
  89.1 0.0 copy-done.4
  89.1 0.0 copy-done.5
  89.2 0.0 copy-done.2
  89.2 0.0 copy-done.3
  89.2 0.7 copy-done.1
  89.9 20.4 %backward.1 = (f32[16,48,768]{2,1,0:T(8,128)}, f32[16,48,768]{2,1,0:T(8,128)}, f32[16,48,768]{2,1,0:T(8,128)}, f32[16,48,768]{2,1,0:T(8,128)}) custom-call(bf16[16,48,768]{2,1,0:T(8,128)(2,1)} %u.3, bf16[16,48,768]{2,1,0:T(8,128)(2,1)} %v.3, bf16[16,48,768]{2,1,0:T(8,128)(2,1)} %w.3, bf16[48,768]{1,0:T(8,128)(2,1)} %copy-done.3, bf16[48,768]{1,0:T(8,128)(2,1)} %copy-done.2, ...), custom_call_target="tpu_custom_call" | custom-call | flops 5888802816 | bytes 16865280 | tf_op jit(solution)/shard_map/backward/pallas_call | solution.py:290
  (2 shorter events, 0.0 us)
Async XLA Ops:
  21.0 34.2 %all-to-all-start = ((f32[256,3,1,128]{3,2,1,0:T(1,128)}), f32[256,3,1,128]{3,2,1,0:T(1,128)S(1)}, u32[]{:S(2)}, u32[]{:S(2)}) async-start(f32[256,3,1,128]{3,2,1,0:T(1,128)} %bitcast.17), calls=%async_computation | async-start | bytes 786432 | tf_op jit(solution)/shard_map/all_to_all | solution.py:332
  55.2 0.7 copy-start
  65.1 24.1 %all-to-all-start.1 = ((f32[256,3,1,128]{3,2,1,0:T(1,128)}), f32[256,3,1,128]{3,2,1,0:T(1,128)S(1)}, u32[]{:S(2)}, u32[]{:S(2)}) async-start(f32[256,3,1,128]{3,2,1,0:T(1,128)} %bitcast.14), calls=%async_computation.1 | async-start | bytes 786432 | tf_op jit(solution)/shard_map/all_to_all | solution.py:351
  71.4 16.4 %collective-permute-start.1 = (bf16[48,768]{1,0:T(8,128)(2,1)S(1)}, bf16[48,768]{1,0:T(8,128)(2,1)S(1)}, u32[]{:S(2)}, u32[]{:S(2)}) collective-permute-start(bf16[48,768]{1,0:T(8,128)(2,1)S(1)} %get-tuple-element.10), channel_id=1, source_target_pairs={{0,248},{8,0},{16,8},{24,16},{32,24},{40,32},{48,40},{56,48},{64,5... | collective-permute-start | bytes 221192 | tf_op jit(solution)/shard_map/ppermute | solution.py:285
  73.8 14.0 %collective-permute-start = (bf16[48,768]{1,0:T(8,128)(2,1)S(1)}, bf16[48,768]{1,0:T(8,128)(2,1)S(1)}, u32[]{:S(2)}, u32[]{:S(2)}) collective-permute-start(bf16[48,768]{1,0:T(8,128)(2,1)S(1)} %get-tuple-element.11), channel_id=1, source_target_pairs={{0,8},{8,16},{16,24},{24,32},{32,40},{40,48},{48,56},{56,64},{64,7... | collective-permute-start | bytes 221192 | tf_op jit(solution)/shard_map/ppermute | solution.py:285
  74.9 12.3 %collective-permute-start.2 = (bf16[16,768]{1,0:T(8,128)(2,1)S(1)}, bf16[16,768]{1,0:T(8,128)(2,1)S(1)}, u32[]{:S(2)}, u32[]{:S(2)}) collective-permute-start(bf16[16,768]{1,0:T(8,128)(2,1)S(1)} %bitcast.18), channel_id=1, source_target_pairs={{0,1},{1,2},{2,3},{3,4},{4,5},{5,6},{6,7},{7,0},{8,9},{9,10},{10,1... | collective-permute-start | bytes 73736 | tf_op jit(solution)/shard_map/ppermute | solution.py:285
  80.8 7.0 %collective-permute-start.3 = (bf16[16,768]{1,0:T(8,128)(2,1)S(1)}, bf16[16,768]{1,0:T(8,128)(2,1)S(1)}, u32[]{:S(2)}, u32[]{:S(2)}) collective-permute-start(bf16[16,768]{1,0:T(8,128)(2,1)S(1)} %bitcast.19), channel_id=1, source_target_pairs={{0,7},{1,0},{2,1},{3,2},{4,3},{5,4},{6,5},{7,6},{8,15},{9,8},{10,9... | collective-permute-start | bytes 73736 | tf_op jit(solution)/shard_map/ppermute | solution.py:285
  87.2 1.9 %copy-start.4 = (bf16[16,768]{1,0:T(8,128)(2,1)}, bf16[16,768]{1,0:T(8,128)(2,1)S(1)}, u32[]{:S(2)}) copy-start(bf16[16,768]{1,0:T(8,128)(2,1)S(1)} %collective-permute-done.2.wl) | copy-start | bytes 73732
  87.8 1.3 %copy-start.5 = (bf16[16,768]{1,0:T(8,128)(2,1)}, bf16[16,768]{1,0:T(8,128)(2,1)S(1)}, u32[]{:S(2)}) copy-start(bf16[16,768]{1,0:T(8,128)(2,1)S(1)} %collective-permute-done.3.wh) | copy-start | bytes 73732
  87.8 1.3 %copy-start.2 = (bf16[48,768]{1,0:T(8,128)(2,1)}, bf16[48,768]{1,0:T(8,128)(2,1)S(1)}, u32[]{:S(2)}) copy-start(bf16[48,768]{1,0:T(8,128)(2,1)S(1)} %collective-permute-done.1.uh) | copy-start | bytes 221188
  87.8 1.3 %copy-start.3 = (bf16[48,768]{1,0:T(8,128)(2,1)}, bf16[48,768]{1,0:T(8,128)(2,1)S(1)}, u32[]{:S(2)}) copy-start(bf16[48,768]{1,0:T(8,128)(2,1)S(1)} %collective-permute-done.ul) | copy-start | bytes 221188
  89.1 0.7 copy-start.1
where the time goes:
time: 111 us; the launch traced here: 110 us
  Pallas kernels  49.9 us (45%)
  starting transfers between devices  31.9 us (29%)
  waiting for transfers between devices  23.5 us (21%)
  local copies, waits for them, and re-layouts  4.3 us (4%)
    pallas_call x3, Pallas kernels, call(): pl.pallas_call(kernel, out_shape=outs, in_specs=[pl.BlockSpec(memory_spac...  49.9 us
    all_to_all x1, waiting for transfers between devices, on_device(): lax.all_to_all(send, ('gx', 'gz'), split_axis=0, concat_axis=0, tiled=True)  17.7 us
    all_to_all x1, starting transfers between devices, on_device(): lax.all_to_all(send, ('gx', 'gz'), split_axis=0, concat_axis=0, tiled=True)  15.7 us
    ppermute x4, starting transfers between devices, shifted(): lax.ppermute(block, axis, [(i, (i + step) % count) for i in range(count)])  10.9 us
    all_to_all x1, starting transfers between devices, on_device(): lax.all_to_all(back, ('gx', 'gz'), split_axis=0, concat_axis=0, tiled=True)  5.41 us
    ppermute x4, waiting for transfers between devices, shifted(): lax.ppermute(block, axis, [(i, (i + step) % count) for i in range(count)])  4.41 us
  transfers between devices with their start and end apart: 6, of which 4 were waited for; matrix products, arithmetic and copies ran while one was open for 3% of the time, Pallas kernels for 0%

commit v1 on v0

--- a/solution.py
+++ b/solution.py
@@ -12,6 +12,7 @@
 F32 = jnp.float32
 BF16 = jnp.bfloat16
 TILE = 256
+STRIDE = 37
 LANES = 128
 
 
@@ -120,10 +121,13 @@
 
 
 def forward_kernel(
-    u, v, w, sa, ca, sb, cb, sx, sz, eh, el, mux, mum, send, modes, sh, sl, kh, kl, dh, dl
+    u, v, w, sa, ca, sb, cb, sx, sz, eh, el, mux, mum, send, modes, wlow, whigh,
+    sh, sl, kh, kl, dh, dl
 ):
     cx, cz, ny = u.shape
     cells = cx * cz
+    wlow[...] = w[:, 0, :]
+    whigh[...] = w[:, cz - 1, :]
     fill_sine((sa, ca, sb, cb), sh, sl)
     fill_local(sx, sz, kh, kl)
 
@@ -156,10 +160,87 @@
         send[cols, :] = edge.T
 
 
+def send_blocks(source, target, send_sem, recv_sem, own_sem):
+    ngx, ngz = lax.axis_size("gx"), lax.axis_size("gz")
+    devices = ngx * ngz
+    per = source.shape[0] // devices
+    me = lax.axis_index("gx") * ngz + lax.axis_index("gz")
+    mine = pl.ds(me * per, per)
+
+    def copy(other):
+        return pltpu.make_async_remote_copy(
+            src_ref=source.at[pl.ds(other * per, per)],
+            dst_ref=target.at[mine],
+            send_sem=send_sem,
+            recv_sem=recv_sem,
+            device_id=(other // ngz, other % ngz),
+            device_id_type=pl.DeviceIdType.MESH,
+        )
+
+    def start(k, carry):
+        copy((me + STRIDE * k) % devices).start()
+        return carry
+
+    lax.fori_loop(1, devices, start, 0)
+    own = pltpu.make_async_copy(source.at[mine], target.at[mine], own_sem)
+    own.start()
+    rest = pl.ds(0, (devices - 1) * per)
+    everything = pltpu.make_async_remote_copy(
+        src_ref=source.at[rest],
+        dst_ref=target.at[rest],
+        send_sem=send_sem,
+        recv_sem=recv_sem,
+        device_id=(lax.axis_index("gx"), (lax.axis_index("gz") + 1) % ngz),
+        device_id_type=pl.DeviceIdType.MESH,
+    )
+    return own, everything
+
+
+def exchange_kernel(source, target, send_sem, recv_sem, own_sem):
+    own, everything = send_blocks(source, target, send_sem, recv_sem, own_sem)
+    own.wait()
+    everything.wait_send()
+    everything.wait_recv()
+
+
+def exchange_halo_kernel(
+    source, u, wlow, whigh, target, ul, uh, wl, wh, send_sem, recv_sem, own_sem, hs, hr
+):
+    ngx, ngz = lax.axis_size("gx"), lax.axis_size("gz")
+    gx, gz = lax.axis_index("gx"), lax.axis_index("gz")
+    last = u.shape[0] - 1
+    plan = [
+        (u.at[last], ul, ((gx + 1) % ngx, gz)),
+        (u.at[0], uh, ((gx + ngx - 1) % ngx, gz)),
+        (whigh, wl, (gx, (gz + 1) % ngz)),
+        (wlow, wh, (gx, (gz + ngz - 1) % ngz)),
+    ]
+    copies = [
+        pltpu.make_async_remote_copy(
+            src_ref=a,
+            dst_ref=b,
+            send_sem=hs.at[i],
+            recv_sem=hr.at[i],
+            device_id=to,
+            device_id_type=pl.DeviceIdType.MESH,
+        )
+        for i, (a, b, to) in enumerate(plan)
+    ]
+    own, everything = send_blocks(source, target, send_sem, recv_sem, own_sem)
+    for c in copies:
+        c.start()
+    own.wait()
+    everything.wait_send()
+    everything.wait_recv()
+    for c in copies:
+        c.wait()
+
+
 def owner_kernel(
     ngx, ngz, cx, cz, seen, hxh, hxl, hzh, hzl, lxh, lxl, lxth, lxtl, lzth, lztl, muz, mukx, mum, out
 ):
-    per = mum.shape[0]
+    per = mum.shape[0] // (ngx * ngz)
+    me = lax.axis_index("gx") * ngz + lax.axis_index("gz")
     nx, nz = ngx * cx, ngz * cz
     lane = lax.broadcasted_iota(jnp.int32, (ngx, LANES), 1)
     lane8 = lax.broadcasted_iota(jnp.int32, (ngz, LANES), 1)
@@ -194,7 +275,7 @@
         mine = f1[2 * ngx * m : 2 * ngx * (m + 1)]
         other = f2[2 * ngz * m : 2 * ngz * (m + 1)].T
         spec = dot3((lxh[...], lxl[...]), split(mine)) + dot3(split(other), (lzth[...], lztl[...]))
-        spec = spec / ((mukx[...] + muz[...] + mum[m : m + 1, :1]) * (-float(nx * nz)))
+        spec = spec / ((mukx[...] + muz[...] + mum[me * per + m]) * (-float(nx * nz)))
         spec = split(spec)
         ex.append(dot3((lxth[...], lxtl[...]), spec))
         ez.append(dot3((lzth[...], lztl[...]), spec, dot_t))
@@ -280,20 +361,20 @@
         finish(x, pressure[x - 1], pressure[x + 1])
 
 
-def shifted(block, axis, step):
-    count = lax.axis_size(axis)
-    return lax.ppermute(block, axis, [(i, (i + step) % count) for i in range(count)])
-
-
-def call(kernel, name, outs, scratch, flops, *args):
+def call(kernel, name, outs, scratch, flops, *args, places=(), effects=False):
+    spaces = dict(places)
     size = sum(math.prod(a.shape) * a.dtype.itemsize for a in [*args, *outs])
     return pl.pallas_call(
         kernel,
         out_shape=outs,
-        in_specs=[pl.BlockSpec(memory_space=pltpu.VMEM)] * len(args),
+        in_specs=[
+            pl.BlockSpec(memory_space=spaces.get(i, pltpu.VMEM)) for i in range(len(args))
+        ],
         out_specs=[pl.BlockSpec(memory_space=pltpu.VMEM)] * len(outs),
         scratch_shapes=scratch,
-        compiler_params=pltpu.CompilerParams(vmem_limit_bytes=60 << 20),
+        compiler_params=pltpu.CompilerParams(
+            vmem_limit_bytes=60 << 20, has_side_effects=effects
+        ),
         cost_estimate=pl.CostEstimate(flops=flops, bytes_accessed=size, transcendentals=0),
         name=name,
     )(*args)
@@ -308,11 +389,6 @@
     per = ny // devices
     cells = cx * cz
     edges = 2 * (cx + cz)
-    me = lax.axis_index("gx") * ngz + lax.axis_index("gz")
-    u_low = shifted(u_vel[-1], "gx", 1)
-    u_high = shifted(u_vel[0], "gx", -1)
-    w_low = shifted(w_vel[:, -1], "gz", 1)
-    w_high = shifted(w_vel[:, 0], "gz", -1)
     local = np.kron(sine_np(cx), sine_np(cz))[edge_rows(cx, cz)]
     tables = [f32(t) for t in sine_parts_np(ny, 32)]
     tables += [f32(np.repeat(sine_np(cx), cz, 1)), f32(np.tile(sine_np(cz), (1, cx)))]
@@ -320,21 +396,31 @@
     mum = f32(wall_eigen_np(ny).reshape(1, -1))
     shape = jax.ShapeDtypeStruct
     square = [pltpu.VMEM((ny, ny), BF16)] * 2 + [pltpu.VMEM((cells, cells), BF16)] * 2
-    send, modes = call(
+    u_edge, w_edge = shape((cz, ny), BF16), shape((cx, ny), BF16)
+    send, modes, w_first, w_last = call(
         forward_kernel,
         "forward",
-        [shape((ny, edges), F32), shape((cells, ny), F32)],
+        [shape((ny, edges), F32), shape((cells, ny), F32), w_edge, w_edge],
         square + [pltpu.VMEM((cells + edges, ny), BF16), pltpu.VMEM((cells, ny), BF16)],
         6 * cells * ny * (ny + cells + edges),
         u_vel, v_vel, w_vel, *tables, *halves(local), mux, mum,
     )
-    send = send.reshape(devices, per, 1, edges)
-    seen = lax.all_to_all(send, ("gx", "gz"), split_axis=0, concat_axis=0, tiled=True)
+    rows = shape((ny, 1, edges), F32)
+    sems = [pltpu.SemaphoreType.DMA] * 3
+    seen, u_low, u_high, w_low, w_high = call(
+        exchange_halo_kernel,
+        "exchange_halo",
+        [rows, u_edge, u_edge, w_edge, w_edge],
+        sems + [pltpu.SemaphoreType.DMA((4,))] * 2,
+        0,
+        send.reshape(ny, 1, edges), u_vel, w_first, w_last,
+        places={1: pl.ANY},
+        effects=True,
+    )
     hx, hz = hartley_np(nx), hartley_np(nz)
     block_x, block_z = np.arange(ngx) * cx, np.arange(ngz) * cz
     lx = hx[:, np.concatenate([(block_x - 1) % nx, (block_x + cx) % nx])]
     lz = hz[:, np.concatenate([(block_z - 1) % nz, (block_z + cz) % nz])]
-    lam_m = lax.dynamic_slice(jnp.asarray(mum[0]), (me * per,), (per,))
     (back,) = call(
         functools.partial(owner_kernel, ngx, ngz, cx, cz),
         "owner",
@@ -345,10 +431,12 @@
         *halves(hx), *halves(hz), *halves(lx), *halves(lx.T), *halves(lz.T),
         f32(periodic_eigen_np(nz).reshape(1, -1)),
         f32(periodic_eigen_np(nx).reshape(-1, 1)),
-        jnp.broadcast_to(lam_m[:, None], (per, LANES)),
-    )
-    back = back.reshape(devices, per, 1, edges)
-    got = lax.all_to_all(back, ("gx", "gz"), split_axis=0, concat_axis=0, tiled=True)
+        f32(mum[0]),
+        places={13: pltpu.SMEM},
+    )
+    (got,) = call(
+        exchange_kernel, "exchange", [rows], sems, 0, back.reshape(ny, 1, edges), effects=True
+    )
     block = shape((cx, cz, ny), F32)
     return tuple(
         call(

time: 111 us -> 114 us (1.027)
  Pallas kernels: 49.9 us -> 113 us
  starting transfers between devices: 31.9 us -> 0 us
  waiting for transfers between devices: 23.5 us -> 0 us
  local copies, waits for them, and re-layouts: 4.3 us -> 0 us
    pallas_call x3 -> x5, Pallas kernels: 49.9 us -> 113 us  [call(): pl.pallas_call(kernel, out_shape=outs, in_specs=[pl.BlockSpec(memory_spac...]
    all_to_all x2 -> x0, starting transfers between devices: 21.1 us -> none  [the longest x1 15.7 us: on_device(): lax.all_to_all(send, ('gx', 'gz'), split_axis=0, concat_axis=0, tiled=True)]
    all_to_all x2 -> x0, waiting for transfers between devices: 19.1 us -> none  [the longest x1 17.7 us: on_device(): lax.all_to_all(send, ('gx', 'gz'), split_axis=0, concat_axis=0, tiled=True)]
    ppermute x4 -> x0, starting transfers between devices: 10.9 us -> none  [shifted(): lax.ppermute(block, axis, [(i, (i + step) % count) for i in range(count)])]
    ppermute x4 -> x0, waiting for transfers between devices: 4.41 us -> none  [shifted(): lax.ppermute(block, axis, [(i, (i + step) % count) for i in range(count)])]
  transfers between devices with their start and end apart: 6 -> 0, of which waited for: 4 -> 0; matrix products, arithmetic and copies ran while one was open for 3% -> 0% of each run, Pallas kernels for 0% -> 0%
where the time goes in v1:
time: 114 us
  Pallas kernels  113 us (99%)
    pallas_call x5, Pallas kernels, call(): pl.pallas_call(kernel, out_shape=outs, in_specs=[pl.BlockSpec(memory_spac...  113 us

profile of v1, /device:TPU:1, one launch (start us, length us, event | category | flops | bytes accessed | tf_op | source)
XLA Modules:
  0.0 113.9 jit_solution(7355629199531428481)
XLA Ops:
  0.6 20.4 %forward.1 = (f32[768,128]{1,0:T(8,128)}, f32[768,768]{1,0:T(8,128)}, bf16[16,768]{1,0:T(8,128)(2,1)}, bf16[16,768]{1,0:T(8,128)(2,1)}) custom-call(bf16[16,48,768]{2,1,0:T(8,128)(2,1)} %u.5, bf16[16,48,768]{2,1,0:T(8,128)(2,1)} %v.3, bf16[16,48,768]{2,1,0:T(8,128)(2,1)} %w.3, f32[24,768]{1,0:T(8,128)} %constant.50.clone.sa, f32[24,768]{1,0:T(8,128)} %constant.51.clone.ca, ...), custom_call_target="tpu_custom_call" | custom-call | flops 5888802816 | bytes 7280640 | tf_op jit(solution)/shard_map/forward/pallas_call | solution.py:367
  21.1 35.6 %exchange_halo.1 = (f32[768,1,128]{2,1,0:T(1,128)}, bf16[48,768]{1,0:T(8,128)(2,1)}, bf16[48,768]{1,0:T(8,128)(2,1)}, bf16[16,768]{1,0:T(8,128)(2,1)}, bf16[16,768]{1,0:T(8,128)(2,1)}) custom-call(f32[768,1,128]{2,1,0:T(1,128)} %bitcast.7, bf16[16,48,768]{2,1,0:T(8,128)(2,1)} %u.5, bf16[16,768]{1,0:T(8,128)(2,1)} %get-tuple-element.14.wlow, ...), custom_call_target="tpu_custom_call" | custom-call | bytes 2211840 | tf_op jit(solution)/shard_map/exchange_halo/pallas_call | solution.py:367
  56.7 9.0 %owner.1 = f32[768,128]{1,0:T(8,128)} custom-call(f32[768,128]{1,0:T(8,128)} %bitcast.5, bf16[512,512]{1,0:T(8,128)(2,1)} %constant.60.clone.hxh, bf16[512,512]{1,0:T(8,128)(2,1)} %constant.61.clone.hxl, bf16[384,384]{1,0:T(8,128)(2,1)} %constant.62.clone.hzh, bf16[384,384]{1,0:T(8,128)(2,1)} %constant.63.clone.hzl, bf16[512,64]{1,0:T(8,128)(2,1)} %constant.64.clone.lxh, ...), custom_call_target="tpu_custom_call" | custom-call | flops 707788800 | bytes 2718208 | tf_op jit(solution)/shard_map/owner/pallas_call | solution.py:367
  65.6 27.8 %exchange.1 = f32[768,1,128]{2,1,0:T(1,128)} custom-call(f32[768,1,128]{2,1,0:T(1,128)} %bitcast.4), custom_call_target="tpu_custom_call" | custom-call | bytes 786432 | tf_op jit(solution)/shard_map/exchange/pallas_call | solution.py:367
  93.5 20.4 %backward.1 = (f32[16,48,768]{2,1,0:T(8,128)}, f32[16,48,768]{2,1,0:T(8,128)}, f32[16,48,768]{2,1,0:T(8,128)}, f32[16,48,768]{2,1,0:T(8,128)}) custom-call(bf16[16,48,768]{2,1,0:T(8,128)(2,1)} %u.5, bf16[16,48,768]{2,1,0:T(8,128)(2,1)} %v.3, bf16[16,48,768]{2,1,0:T(8,128)(2,1)} %w.3, bf16[48,768]{1,0:T(8,128)(2,1)} %get-tuple-element.16.ul, ...), custom_call_target="tpu_custom_call" | custom-call | flops 5888802816 | bytes 16865280 | tf_op jit(solution)/shard_map/backward/pallas_call | solution.py:367

commit v2 on v0

--- a/solution.py
+++ b/solution.py
@@ -119,13 +119,29 @@
     return up - down
 
 
+def arrivals(pairs, sems):
+    copies = [pltpu.make_async_copy(a, b, sems.at[i]) for i, (a, b) in enumerate(pairs)]
+    for c in copies:
+        c.start()
+    return copies
+
+
+def tile_copy(source, target, sems, n):
+    cols = pl.ds(pl.multiple_of(n * TILE, TILE), TILE)
+    return pltpu.make_async_copy(source.at[..., cols], target.at[..., cols], sems.at[n])
+
+
 def forward_kernel(
-    u, v, w, sa, ca, sb, cb, sx, sz, eh, el, mux, mum, send, modes, sh, sl, kh, kl, dh, dl
+    u_hbm, v_hbm, w_hbm, sa, ca, sb, cb, sx, sz, eh, el, mux, mum, send, modes_hbm,
+    sh, sl, kh, kl, dh, dl, u, v, w, modes, in_sem, out_sem,
 ):
     cx, cz, ny = u.shape
     cells = cx * cz
+    arrive = arrivals([(u_hbm, u), (v_hbm, v), (w_hbm, w)], in_sem)
     fill_sine((sa, ca, sb, cb), sh, sl)
     fill_local(sx, sz, kh, kl)
+    for c in arrive:
+        c.wait()
 
     @pl.loop(0, cx)
     def _(x):
@@ -154,6 +170,11 @@
         mode = mode / (mux[...] + mum[:, cols])
         edge = wide[cells:] - dot3((eh[...], el[...]), split(mode))
         send[cols, :] = edge.T
+        tile_copy(modes, modes_hbm, out_sem, n).start()
+
+    @pl.loop(0, ny // TILE)
+    def _(n):
+        tile_copy(modes, modes_hbm, out_sem, n).wait()
 
 
 def owner_kernel(
@@ -232,13 +253,17 @@
 
 
 def backward_kernel(
-    u, v, w, ul, uh, wl, wh, got, modes, sa, ca, sb, cb, sx, sz, eth, etl, mux, mum,
-    pressure, u_new, v_new, w_new, sh, sl, kh, kl, fh, fl, ring, plow, phigh,
+    u_hbm, v_hbm, w_hbm, ul, uh, wl, wh, got, modes_hbm, sa, ca, sb, cb, sx, sz, eth, etl, mux, mum,
+    pressure_hbm, u_out, v_out, w_out, sh, sl, kh, kl, fh, fl, ring, plow, phigh,
+    u, v, w, modes, pressure, u_new, v_new, w_new, in_sem, p_sem, out_sem,
 ):
     cx, cz, ny = u.shape
     cells = cx * cz
+    arrive = arrivals([(modes_hbm, modes), (u_hbm, u), (v_hbm, v), (w_hbm, w)], in_sem)
     fill_sine((sa, ca, sb, cb), sh, sl)
     fill_local(sx, sz, kh, kl)
+
+    arrive[0].wait()
 
     @pl.loop(0, ny // TILE)
     def _(n):
@@ -257,6 +282,13 @@
         pressure[:, :, cols] = wide[:cells].reshape(cx, cz, TILE)
         ring[:, cols] = wide[cells:]
 
+        @pl.when(n > 0)
+        def _():
+            tile_copy(pressure, pressure_hbm, p_sem, n - 1).start()
+
+    for c in arrive[1:]:
+        c.wait()
+
     plow[...] = ring[:cz, :] - 0.5 * ul[...].astype(F32)
     phigh[...] = ring[cz : 2 * cz, :] + 0.5 * uh[...].astype(F32)
     edge = pl.ds(2 * cz, cx)
@@ -272,12 +304,39 @@
         last = ring[pl.ds(2 * cz + cx + x, 1), :]
         w_new[x] = w[x].astype(F32) - 0.5 * along_rows(here, first, last)
 
+    def leave(x):
+        planes = [(u_new, u_out), (v_new, v_out), (w_new, w_out)]
+        return [
+            pltpu.make_async_copy(a.at[x], b.at[x], out_sem.at[i, x])
+            for i, (a, b) in enumerate(planes)
+        ]
+
     finish(0, plow[...], pressure[1])
     finish(cx - 1, pressure[cx - 2], phigh[...])
+    tile_copy(pressure, pressure_hbm, p_sem, ny // TILE - 1).start()
 
     @pl.loop(1, cx - 1)
     def _(x):
         finish(x, pressure[x - 1], pressure[x + 1])
+        for c in leave(x - 1):
+            c.start()
+
+    for x in (cx - 1, cx - 2):
+        for c in leave(x):
+            c.start()
+
+    @pl.loop(0, ny // TILE)
+    def _(n):
+        tile_copy(pressure, pressure_hbm, p_sem, n).wait()
+
+    @pl.loop(0, cx)
+    def _(x):
+        for c in leave(x):
+            c.wait()
+
+
+def _(x):
+        finish(x, pressure[x - 1], pressure[x + 1])
 
 
 def shifted(block, axis, step):
@@ -285,13 +344,18 @@
     return lax.ppermute(block, axis, [(i, (i + step) % count) for i in range(count)])
 
 
-def call(kernel, name, outs, scratch, flops, *args):
+def call(kernel, name, outs, scratch, flops, *args, places=(), out_places=()):
+    spaces, out_spaces = dict(places), dict(out_places)
     size = sum(math.prod(a.shape) * a.dtype.itemsize for a in [*args, *outs])
     return pl.pallas_call(
         kernel,
         out_shape=outs,
-        in_specs=[pl.BlockSpec(memory_space=pltpu.VMEM)] * len(args),
-        out_specs=[pl.BlockSpec(memory_space=pltpu.VMEM)] * len(outs),
+        in_specs=[
+            pl.BlockSpec(memory_space=spaces.get(i, pltpu.VMEM)) for i in range(len(args))
+        ],
+        out_specs=[
+            pl.BlockSpec(memory_space=out_spaces.get(i, pltpu.VMEM)) for i in range(len(outs))
+        ],
         scratch_shapes=scratch,
         compiler_params=pltpu.CompilerParams(vmem_limit_bytes=60 << 20),
         cost_estimate=pl.CostEstimate(flops=flops, bytes_accessed=size, transcendentals=0),
@@ -320,13 +384,20 @@
     mum = f32(wall_eigen_np(ny).reshape(1, -1))
     shape = jax.ShapeDtypeStruct
     square = [pltpu.VMEM((ny, ny), BF16)] * 2 + [pltpu.VMEM((cells, cells), BF16)] * 2
+    planes = [pltpu.VMEM((cx, cz, ny), BF16)] * 3
     send, modes = call(
         forward_kernel,
         "forward",
         [shape((ny, edges), F32), shape((cells, ny), F32)],
-        square + [pltpu.VMEM((cells + edges, ny), BF16), pltpu.VMEM((cells, ny), BF16)],
+        square
+        + [pltpu.VMEM((cells + edges, ny), BF16), pltpu.VMEM((cells, ny), BF16)]
+        + planes
+        + [pltpu.VMEM((cells, ny), F32)]
+        + [pltpu.SemaphoreType.DMA((3,)), pltpu.SemaphoreType.DMA((ny // TILE,))],
         6 * cells * ny * (ny + cells + edges),
         u_vel, v_vel, w_vel, *tables, *halves(local), mux, mum,
+        places={i: pl.ANY for i in range(3)},
+        out_places={1: pl.ANY},
     )
     send = send.reshape(devices, per, 1, edges)
     seen = lax.all_to_all(send, ("gx", "gz"), split_axis=0, concat_axis=0, tiled=True)
@@ -358,10 +429,17 @@
             square
             + [pltpu.VMEM((cells + edges, ny), BF16)] * 2
             + [pltpu.VMEM((edges, ny), F32)]
-            + [pltpu.VMEM((cz, ny), F32)] * 2,
+            + [pltpu.VMEM((cz, ny), F32)] * 2
+            + planes
+            + [pltpu.VMEM((cells, ny), F32)]
+            + [pltpu.VMEM((cx, cz, ny), F32)] * 4
+            + [pltpu.SemaphoreType.DMA((4,)), pltpu.SemaphoreType.DMA((ny // TILE,))]
+            + [pltpu.SemaphoreType.DMA((3, cx))],
             6 * cells * ny * (ny + cells + edges),
             u_vel, v_vel, w_vel, u_low, u_high, w_low, w_high, got.reshape(ny, edges), modes,
             *tables, *halves(local.T), mux, mum,
+            places={i: pl.ANY for i in (0, 1, 2, 8)},
+            out_places={i: pl.ANY for i in range(4)},
         )
     )
 

time: 111 us -> 108 us (0.973)
  Pallas kernels: 49.9 us -> 46.7 us
    pallas_call x3, Pallas kernels: 49.9 us -> 46.7 us  [call(): pl.pallas_call(kernel, out_shape=outs, in_specs=[pl.BlockSpec(memory_spac...]
where the time goes in v2:
time: 108 us; the launch traced here: 107 us
  Pallas kernels  46.7 us (43%)
  starting transfers between devices  31.9 us (30%)
  waiting for transfers between devices  23.5 us (22%)
  local copies, waits for them, and re-layouts  4.3 us (4%)
    pallas_call x3, Pallas kernels, call(): pl.pallas_call(kernel, out_shape=outs, in_specs=[pl.BlockSpec(memory_spac...  46.7 us
    all_to_all x1, waiting for transfers between devices, on_device(): lax.all_to_all(send, ('gx', 'gz'), split_axis=0, concat_axis=0, tiled=True)  17.7 us
    all_to_all x1, starting transfers between devices, on_device(): lax.all_to_all(send, ('gx', 'gz'), split_axis=0, concat_axis=0, tiled=True)  15.7 us
    ppermute x4, starting transfers between devices, shifted(): lax.ppermute(block, axis, [(i, (i + step) % count) for i in range(count)])  10.9 us
    all_to_all x1, starting transfers between devices, on_device(): lax.all_to_all(back, ('gx', 'gz'), split_axis=0, concat_axis=0, tiled=True)  5.42 us
    ppermute x4, waiting for transfers between devices, shifted(): lax.ppermute(block, axis, [(i, (i + step) % count) for i in range(count)])  4.41 us
  transfers between devices with their start and end apart: 6, of which 4 were waited for; matrix products, arithmetic and copies ran while one was open for 3% of the time, Pallas kernels for 0%

profile of v2, /device:TPU:1, one launch (start us, length us, event | category | flops | bytes accessed | tf_op | source)
XLA Modules:
  0.0 107.2 jit_solution(13658273545518525603)
XLA Ops:
  0.6 20.4 %forward.1 = (f32[768,128]{1,0:T(8,128)}, f32[768,768]{1,0:T(8,128)}) custom-call(bf16[16,48,768]{2,1,0:T(8,128)(2,1)} %u_hbm.3, bf16[16,48,768]{2,1,0:T(8,128)(2,1)} %v_hbm.3, bf16[16,48,768]{2,1,0:T(8,128)(2,1)} %w_hbm.3, f32[24,768]{1,0:T(8,128)} %constant.67.clone.sa, f32[24,768]{1,0:T(8,128)} %constant.68.clone.ca, f32[32,768]{1,0:T(8,128)} %constant.69.clone.sb, ...), custom_call_target="tpu_custom_call" | custom-call | flops 5888802816 | bytes 7231488 | tf_op jit(solution)/shard_map/forward/pallas_call | solution.py:350
  21.0 15.7 %all-to-all-start = ((f32[256,3,1,128]{3,2,1,0:T(1,128)}), f32[256,3,1,128]{3,2,1,0:T(1,128)S(1)}, u32[]{:S(2)}, u32[]{:S(2)}) async-start(f32[256,3,1,128]{3,2,1,0:T(1,128)} %bitcast.17), calls=%async_computation | async-start | bytes 786432 | tf_op jit(solution)/shard_map/all_to_all | solution.py:403
  36.7 0.8 dynamic_slice.3
  37.5 17.7 %all-to-all-done = f32[256,3,1,128]{3,2,1,0:T(1,128)S(1)} async-done(((f32[256,3,1,128]{3,2,1,0:T(1,128)}), f32[256,3,1,128]{3,2,1,0:T(1,128)S(1)}, u32[]{:S(2)}, u32[]{:S(2)}) %all-to-all-start) | async-done | bytes 393248 | tf_op jit(solution)/shard_map/all_to_all | solution.py:403
  55.2 0.0 copy-start
  55.2 0.7 broadcast_in_dim.2.mum
  55.9 0.0 copy-done
  56.0 9.1 %owner.1 = f32[768,128]{1,0:T(8,128)} custom-call(f32[768,128]{1,0:T(8,128)} %bitcast.15, bf16[512,512]{1,0:T(8,128)(2,1)} %constant.78.clone.hxh, bf16[512,512]{1,0:T(8,128)(2,1)} %constant.79.clone.hxl, bf16[384,384]{1,0:T(8,128)(2,1)} %constant.80.clone.hzh, bf16[384,384]{1,0:T(8,128)(2,1)} %constant.81.clone.hzl, bf16[512,64]{1,0:T(8,128)(2,1)} %constant.82.clone.lxh, ...), custom_call_target="tpu_custom_call" | custom-call | flops 707788800 | bytes 2716672 | tf_op jit(solution)/shard_map/owner/pallas_call | solution.py:350
  65.1 5.4 %all-to-all-start.1 = ((f32[256,3,1,128]{3,2,1,0:T(1,128)}), f32[256,3,1,128]{3,2,1,0:T(1,128)S(1)}, u32[]{:S(2)}, u32[]{:S(2)}) async-start(f32[256,3,1,128]{3,2,1,0:T(1,128)} %bitcast.14), calls=%async_computation.1 | async-start | bytes 786432 | tf_op jit(solution)/shard_map/all_to_all | solution.py:422
  70.5 0.9 slice_bitcast_fusion
  71.5 2.4 %collective-permute-start.1 = (bf16[48,768]{1,0:T(8,128)(2,1)S(1)}, bf16[48,768]{1,0:T(8,128)(2,1)S(1)}, u32[]{:S(2)}, u32[]{:S(2)}) collective-permute-start(bf16[48,768]{1,0:T(8,128)(2,1)S(1)} %get-tuple-element.10), channel_id=1, source_target_pairs={{0,248},{8,0},{16,8},{24,16},{32,24},{40,32},{48,40},{56,48},{64,5... | collective-permute-start | bytes 221192 | tf_op jit(solution)/shard_map/ppermute | solution.py:344
  73.8 0.0 collective-permute-start
  73.8 1.1 %fusion = (bf16[16,1,768]{2,1,0:T(2,128)(2,1)S(1)}, bf16[16,1,768]{2,1,0:T(2,128)(2,1)S(1)}) fusion(bf16[16,48,768]{2,1,0:T(8,128)(2,1)} %w_hbm.3), kind=kLoop, calls=%fused_computation.4 | loop fusion | bytes 98304 | tf_op jit(solution)/shard_map/slice | solution.py:379
  74.9 5.9 %collective-permute-start.2 = (bf16[16,768]{1,0:T(8,128)(2,1)S(1)}, bf16[16,768]{1,0:T(8,128)(2,1)S(1)}, u32[]{:S(2)}, u32[]{:S(2)}) collective-permute-start(bf16[16,768]{1,0:T(8,128)(2,1)S(1)} %bitcast.18), channel_id=1, source_target_pairs={{0,1},{1,2},{2,3},{3,4},{4,5},{5,6},{6,7},{7,0},{8,9},{9,10},{10,1... | collective-permute-start | bytes 73736 | tf_op jit(solution)/shard_map/ppermute | solution.py:344
  80.9 2.6 %collective-permute-start.3 = (bf16[16,768]{1,0:T(8,128)(2,1)S(1)}, bf16[16,768]{1,0:T(8,128)(2,1)S(1)}, u32[]{:S(2)}, u32[]{:S(2)}) collective-permute-start(bf16[16,768]{1,0:T(8,128)(2,1)S(1)} %bitcast.19), channel_id=1, source_target_pairs={{0,7},{1,0},{2,1},{3,2},{4,3},{5,4},{6,5},{7,6},{8,15},{9,8},{10,9... | collective-permute-start | bytes 73736 | tf_op jit(solution)/shard_map/ppermute | solution.py:344
  83.4 3.8 %collective-permute-done.2.wl = bf16[16,768]{1,0:T(8,128)(2,1)S(1)} collective-permute-done((bf16[16,768]{1,0:T(8,128)(2,1)S(1)}, bf16[16,768]{1,0:T(8,128)(2,1)S(1)}, u32[]{:S(2)}, u32[]{:S(2)}) %collective-permute-start.2) | collective-permute-done | bytes 24608 | tf_op jit(solution)/shard_map/ppermute | solution.py:344
  87.2 0.0 copy-start.4
  87.3 0.6 collective-permute-done.3.wh
  87.8 0.0 copy-start.5
  87.9 0.0 collective-permute-done.1.uh
  87.9 0.0 copy-start.2
  87.9 0.0 collective-permute-done.ul
  87.9 0.0 copy-start.3
  87.9 1.3 %all-to-all-done.1 = f32[256,3,1,128]{3,2,1,0:T(1,128)S(1)} async-done(((f32[256,3,1,128]{3,2,1,0:T(1,128)}), f32[256,3,1,128]{3,2,1,0:T(1,128)S(1)}, u32[]{:S(2)}, u32[]{:S(2)}) %all-to-all-start.1) | async-done | bytes 393248 | tf_op jit(solution)/shard_map/all_to_all | solution.py:422
  89.2 0.0 copy-start.1
  89.2 0.0 copy-done.4
  89.2 0.0 copy-done.5
  89.2 0.0 copy-done.2
  89.2 0.0 copy-done.3
  89.2 0.7 copy-done.1
  89.9 17.1 %backward.1 = (f32[16,48,768]{2,1,0:T(8,128)}, f32[16,48,768]{2,1,0:T(8,128)}, f32[16,48,768]{2,1,0:T(8,128)}, f32[16,48,768]{2,1,0:T(8,128)}) custom-call(bf16[16,48,768]{2,1,0:T(8,128)(2,1)} %u_hbm.3, bf16[16,48,768]{2,1,0:T(8,128)(2,1)} %v_hbm.3, bf16[16,48,768]{2,1,0:T(8,128)(2,1)} %w_hbm.3, bf16[48,768]{1,0:T(8,128)(2,1)} %copy-done.3, ...), custom_call_target="tpu_custom_call" | custom-call | flops 5888802816 | bytes 16865280 | tf_op jit(solution)/shard_map/backward/pallas_call | solution.py:350
  (2 shorter events, 0.0 us)
Async XLA Ops:
  21.0 34.2 %all-to-all-start = ((f32[256,3,1,128]{3,2,1,0:T(1,128)}), f32[256,3,1,128]{3,2,1,0:T(1,128)S(1)}, u32[]{:S(2)}, u32[]{:S(2)}) async-start(f32[256,3,1,128]{3,2,1,0:T(1,128)} %bitcast.17), calls=%async_computation | async-start | bytes 786432 | tf_op jit(solution)/shard_map/all_to_all | solution.py:403
  55.2 0.7 copy-start
  65.1 24.1 %all-to-all-start.1 = ((f32[256,3,1,128]{3,2,1,0:T(1,128)}), f32[256,3,1,128]{3,2,1,0:T(1,128)S(1)}, u32[]{:S(2)}, u32[]{:S(2)}) async-start(f32[256,3,1,128]{3,2,1,0:T(1,128)} %bitcast.14), calls=%async_computation.1 | async-start | bytes 786432 | tf_op jit(solution)/shard_map/all_to_all | solution.py:422
  71.5 16.4 %collective-permute-start.1 = (bf16[48,768]{1,0:T(8,128)(2,1)S(1)}, bf16[48,768]{1,0:T(8,128)(2,1)S(1)}, u32[]{:S(2)}, u32[]{:S(2)}) collective-permute-start(bf16[48,768]{1,0:T(8,128)(2,1)S(1)} %get-tuple-element.10), channel_id=1, source_target_pairs={{0,248},{8,0},{16,8},{24,16},{32,24},{40,32},{48,40},{56,48},{64,5... | collective-permute-start | bytes 221192 | tf_op jit(solution)/shard_map/ppermute | solution.py:344
  73.8 14.0 %collective-permute-start = (bf16[48,768]{1,0:T(8,128)(2,1)S(1)}, bf16[48,768]{1,0:T(8,128)(2,1)S(1)}, u32[]{:S(2)}, u32[]{:S(2)}) collective-permute-start(bf16[48,768]{1,0:T(8,128)(2,1)S(1)} %get-tuple-element.11), channel_id=1, source_target_pairs={{0,8},{8,16},{16,24},{24,32},{32,40},{40,48},{48,56},{56,64},{64,7... | collective-permute-start | bytes 221192 | tf_op jit(solution)/shard_map/ppermute | solution.py:344
  74.9 12.3 %collective-permute-start.2 = (bf16[16,768]{1,0:T(8,128)(2,1)S(1)}, bf16[16,768]{1,0:T(8,128)(2,1)S(1)}, u32[]{:S(2)}, u32[]{:S(2)}) collective-permute-start(bf16[16,768]{1,0:T(8,128)(2,1)S(1)} %bitcast.18), channel_id=1, source_target_pairs={{0,1},{1,2},{2,3},{3,4},{4,5},{5,6},{6,7},{7,0},{8,9},{9,10},{10,1... | collective-permute-start | bytes 73736 | tf_op jit(solution)/shard_map/ppermute | solution.py:344
  80.9 7.0 %collective-permute-start.3 = (bf16[16,768]{1,0:T(8,128)(2,1)S(1)}, bf16[16,768]{1,0:T(8,128)(2,1)S(1)}, u32[]{:S(2)}, u32[]{:S(2)}) collective-permute-start(bf16[16,768]{1,0:T(8,128)(2,1)S(1)} %bitcast.19), channel_id=1, source_target_pairs={{0,7},{1,0},{2,1},{3,2},{4,3},{5,4},{6,5},{7,6},{8,15},{9,8},{10,9... | collective-permute-start | bytes 73736 | tf_op jit(solution)/shard_map/ppermute | solution.py:344
  87.2 1.9 %copy-start.4 = (bf16[16,768]{1,0:T(8,128)(2,1)}, bf16[16,768]{1,0:T(8,128)(2,1)S(1)}, u32[]{:S(2)}) copy-start(bf16[16,768]{1,0:T(8,128)(2,1)S(1)} %collective-permute-done.2.wl) | copy-start | bytes 73732
  87.8 1.3 %copy-start.5 = (bf16[16,768]{1,0:T(8,128)(2,1)}, bf16[16,768]{1,0:T(8,128)(2,1)S(1)}, u32[]{:S(2)}) copy-start(bf16[16,768]{1,0:T(8,128)(2,1)S(1)} %collective-permute-done.3.wh) | copy-start | bytes 73732
  87.9 1.3 %copy-start.2 = (bf16[48,768]{1,0:T(8,128)(2,1)}, bf16[48,768]{1,0:T(8,128)(2,1)S(1)}, u32[]{:S(2)}) copy-start(bf16[48,768]{1,0:T(8,128)(2,1)S(1)} %collective-permute-done.1.uh) | copy-start | bytes 221188
  87.9 1.3 %copy-start.3 = (bf16[48,768]{1,0:T(8,128)(2,1)}, bf16[48,768]{1,0:T(8,128)(2,1)S(1)}, u32[]{:S(2)}) copy-start(bf16[48,768]{1,0:T(8,128)(2,1)S(1)} %collective-permute-done.ul) | copy-start | bytes 221188
  89.2 0.7 copy-start.1

commit v3 on v2

--- a/solution.py
+++ b/solution.py
@@ -103,6 +103,14 @@
         high[rows, :], low[rows, :] = split(sx[pl.ds(a, 1), :] * sz[...])
 
 
+def by_parity(high, low, field):
+    half = field.shape[0] // 2
+    parts = []
+    for part in (slice(0, half), slice(half, 2 * half)):
+        parts.append(dot3((high[part, :], low[part, :]), split(field[part])))
+    return jnp.concatenate(parts, 0)
+
+
 def along_rows(x, first, last):
     rows = x.shape[0]
     at = lax.broadcasted_iota(jnp.int32, x.shape, 0)
@@ -143,17 +151,22 @@
     for c in arrive:
         c.wait()
 
-    @pl.loop(0, cx)
-    def _(x):
+    def divergence(x):
         after = u[jnp.minimum(x + 1, cx - 1)].astype(F32) * jnp.where(x < cx - 1, 1.0, 0.0)
         before = u[jnp.maximum(x - 1, 0)].astype(F32) * jnp.where(x > 0, 1.0, 0.0)
-        div = 0.5 * (
+        return 0.5 * (
             (after - before)
             + along_lanes(v[x].astype(F32))
             + along_rows(w[x].astype(F32), 0.0, 0.0)
         )
+
+    @pl.loop(0, cx // 2)
+    def _(x):
+        left, right = divergence(x), divergence(cx - 1 - x)
         rows = pl.ds(pl.multiple_of(x * cz, cz), cz)
-        dh[rows, :], dl[rows, :] = split(div)
+        dh[rows, :], dl[rows, :] = split(left + right)
+        rows = pl.ds(pl.multiple_of(cells // 2 + x * cz, cz), cz)
+        dh[rows, :], dl[rows, :] = split(left - right)
 
     dh[cells : cells + cz, :] = (-0.5 * u[0].astype(F32)).astype(BF16)
     dh[cells + cz : cells + 2 * cz, :] = (0.5 * u[cx - 1].astype(F32)).astype(BF16)
@@ -165,7 +178,7 @@
         cols = pl.ds(pl.multiple_of(n * TILE, TILE), TILE)
         wide = dot(dh[...], sh[:, cols]) + dot(dh[...], sl[:, cols])
         field = wide[:cells] + dot(dl[...], sh[:, cols])
-        mode = dot3((kh[...], kl[...]), split(field))
+        mode = by_parity(kh, kl, field)
         modes[:, cols] = mode
         mode = mode / (mux[...] + mum[:, cols])
         edge = wide[cells:] - dot3((eh[...], el[...]), split(mode))
@@ -270,8 +283,8 @@
         cols = pl.ds(pl.multiple_of(n * TILE, TILE), TILE)
         edge = split(got[cols, :].T)
         field = dot3((eth[...], etl[...]), edge) - modes[:, cols]
-        field = split(field / (mux[...] + mum[:, cols]))
-        field = split(dot3((kh[...], kl[...]), field))
+        field = field / (mux[...] + mum[:, cols])
+        field = split(by_parity(kh, kl, field))
         fh[:cells, cols], fl[:cells, cols] = field
         fh[cells:, cols], fl[cells:, cols] = edge
 
@@ -279,7 +292,11 @@
     def _(n):
         cols = pl.ds(pl.multiple_of(n * TILE, TILE), TILE)
         wide = dot3((fh[...], fl[...]), (sh[:, cols], sl[:, cols]))
-        pressure[:, :, cols] = wide[:cells].reshape(cx, cz, TILE)
+        even = wide[: cells // 2].reshape(cx // 2, cz, TILE)
+        odd = wide[cells // 2 : cells].reshape(cx // 2, cz, TILE)
+        pressure[: cx // 2, :, cols] = even + odd
+        for x in range(cx // 2):
+            pressure[cx - 1 - x, :, cols] = even[x] - odd[x]
         ring[:, cols] = wide[cells:]
 
         @pl.when(n > 0)
@@ -377,13 +394,19 @@
     u_high = shifted(u_vel[0], "gx", -1)
     w_low = shifted(w_vel[:, -1], "gz", 1)
     w_high = shifted(w_vel[:, 0], "gz", -1)
-    local = np.kron(sine_np(cx), sine_np(cz))[edge_rows(cx, cz)]
+    sine_x = sine_np(cx)
+    parity = np.arange(cx).reshape(cx // 2, 2).T
+    order = parity.reshape(-1)
+    local = np.kron(sine_x[:, order], sine_np(cz))[edge_rows(cx, cz)]
     tables = [f32(t) for t in sine_parts_np(ny, 32)]
-    tables += [f32(np.repeat(sine_np(cx), cz, 1)), f32(np.tile(sine_np(cz), (1, cx)))]
-    mux = f32(np.add.outer(wall_eigen_np(cx), wall_eigen_np(cz)).reshape(-1, 1))
+    near = sine_x[: cx // 2]
+    to_modes = np.repeat(near[:, order].T, cz, 1)
+    to_cells = np.repeat(np.concatenate([near[:, p] for p in parity]), cz, 1)
+    along_z = f32(np.tile(sine_np(cz), (1, cx // 2)))
+    mux = f32(np.add.outer(wall_eigen_np(cx)[order], wall_eigen_np(cz)).reshape(-1, 1))
     mum = f32(wall_eigen_np(ny).reshape(1, -1))
     shape = jax.ShapeDtypeStruct
-    square = [pltpu.VMEM((ny, ny), BF16)] * 2 + [pltpu.VMEM((cells, cells), BF16)] * 2
+    square = [pltpu.VMEM((ny, ny), BF16)] * 2 + [pltpu.VMEM((cells, cells // 2), BF16)] * 2
     planes = [pltpu.VMEM((cx, cz, ny), BF16)] * 3
     send, modes = call(
         forward_kernel,
@@ -395,7 +418,7 @@
         + [pltpu.VMEM((cells, ny), F32)]
         + [pltpu.SemaphoreType.DMA((3,)), pltpu.SemaphoreType.DMA((ny // TILE,))],
         6 * cells * ny * (ny + cells + edges),
-        u_vel, v_vel, w_vel, *tables, *halves(local), mux, mum,
+        u_vel, v_vel, w_vel, *tables, f32(to_modes), along_z, *halves(local), mux, mum,
         places={i: pl.ANY for i in range(3)},
         out_places={1: pl.ANY},
     )
@@ -437,7 +460,7 @@
             + [pltpu.SemaphoreType.DMA((3, cx))],
             6 * cells * ny * (ny + cells + edges),
             u_vel, v_vel, w_vel, u_low, u_high, w_low, w_high, got.reshape(ny, edges), modes,
-            *tables, *halves(local.T), mux, mum,
+            *tables, f32(to_cells), along_z, *halves(local.T), mux, mum,
             places={i: pl.ANY for i in (0, 1, 2, 8)},
             out_places={i: pl.ANY for i in range(4)},
         )

time: 108 us -> 103 us (0.954)
  Pallas kernels: 46.7 us -> 41.8 us
    pallas_call x3, Pallas kernels: 46.7 us -> 41.8 us  [call(): pl.pallas_call(kernel, out_shape=outs, in_specs=[pl.BlockSpec(memory_spac...]
where the time goes in v3:
time: 103 us; the launch traced here: 102 us
  Pallas kernels  41.8 us (41%)
  starting transfers between devices  31.9 us (31%)
  waiting for transfers between devices  23.5 us (23%)
  local copies, waits for them, and re-layouts  4.3 us (4%)
    pallas_call x3, Pallas kernels, call(): pl.pallas_call(kernel, out_shape=outs, in_specs=[pl.BlockSpec(memory_spac...  41.8 us
    all_to_all x1, waiting for transfers between devices, on_device(): lax.all_to_all(send, ('gx', 'gz'), split_axis=0, concat_axis=0, tiled=True)  17.7 us
    all_to_all x1, starting transfers between devices, on_device(): lax.all_to_all(send, ('gx', 'gz'), split_axis=0, concat_axis=0, tiled=True)  15.7 us
    ppermute x4, starting transfers between devices, shifted(): lax.ppermute(block, axis, [(i, (i + step) % count) for i in range(count)])  10.9 us
    all_to_all x1, starting transfers between devices, on_device(): lax.all_to_all(back, ('gx', 'gz'), split_axis=0, concat_axis=0, tiled=True)  5.43 us
    ppermute x4, waiting for transfers between devices, shifted(): lax.ppermute(block, axis, [(i, (i + step) % count) for i in range(count)])  4.41 us
  transfers between devices with their start and end apart: 6, of which 4 were waited for; matrix products, arithmetic and copies ran while one was open for 3% of the time, Pallas kernels for 0%

profile of v3, /device:TPU:1, one launch (start us, length us, event | category | flops | bytes accessed | tf_op | source)
XLA Modules:
  0.0 102.4 jit_solution(15988200390381139602)
XLA Ops:
  0.6 17.9 %forward.1 = (f32[768,128]{1,0:T(8,128)}, f32[768,768]{1,0:T(8,128)}) custom-call(bf16[16,48,768]{2,1,0:T(8,128)(2,1)} %u_hbm.3, bf16[16,48,768]{2,1,0:T(8,128)(2,1)} %v_hbm.3, bf16[16,48,768]{2,1,0:T(8,128)(2,1)} %w_hbm.3, f32[24,768]{1,0:T(8,128)} %constant.69.clone.sa, f32[24,768]{1,0:T(8,128)} %constant.70.clone.ca, f32[32,768]{1,0:T(8,128)} %constant.71.clone.sb, ...), custom_call_target="tpu_custom_call" | custom-call | flops 5888802816 | bytes 7133184 | tf_op jit(solution)/shard_map/forward/pallas_call | solution.py:367
  18.5 15.7 %all-to-all-start = ((f32[256,3,1,128]{3,2,1,0:T(1,128)}), f32[256,3,1,128]{3,2,1,0:T(1,128)S(1)}, u32[]{:S(2)}, u32[]{:S(2)}) async-start(f32[256,3,1,128]{3,2,1,0:T(1,128)} %bitcast.17), calls=%async_computation | async-start | bytes 786432 | tf_op jit(solution)/shard_map/all_to_all | solution.py:426
  34.2 0.8 dynamic_slice.3
  35.0 17.7 %all-to-all-done = f32[256,3,1,128]{3,2,1,0:T(1,128)S(1)} async-done(((f32[256,3,1,128]{3,2,1,0:T(1,128)}), f32[256,3,1,128]{3,2,1,0:T(1,128)S(1)}, u32[]{:S(2)}, u32[]{:S(2)}) %all-to-all-start) | async-done | bytes 393248 | tf_op jit(solution)/shard_map/all_to_all | solution.py:426
  52.7 0.0 copy-start
  52.7 0.7 broadcast_in_dim.2.mum
  53.4 0.0 copy-done
  53.5 9.1 %owner.1 = f32[768,128]{1,0:T(8,128)} custom-call(f32[768,128]{1,0:T(8,128)} %bitcast.15, bf16[512,512]{1,0:T(8,128)(2,1)} %constant.80.clone.hxh, bf16[512,512]{1,0:T(8,128)(2,1)} %constant.81.clone.hxl, bf16[384,384]{1,0:T(8,128)(2,1)} %constant.82.clone.hzh, bf16[384,384]{1,0:T(8,128)(2,1)} %constant.83.clone.hzl, bf16[512,64]{1,0:T(8,128)(2,1)} %constant.84.clone.lxh, ...), custom_call_target="tpu_custom_call" | custom-call | flops 707788800 | bytes 2716672 | tf_op jit(solution)/shard_map/owner/pallas_call | solution.py:367
  62.6 5.4 %all-to-all-start.1 = ((f32[256,3,1,128]{3,2,1,0:T(1,128)}), f32[256,3,1,128]{3,2,1,0:T(1,128)S(1)}, u32[]{:S(2)}, u32[]{:S(2)}) async-start(f32[256,3,1,128]{3,2,1,0:T(1,128)} %bitcast.14), calls=%async_computation.1 | async-start | bytes 786432 | tf_op jit(solution)/shard_map/all_to_all | solution.py:445
  68.0 0.9 slice_bitcast_fusion
  69.0 2.4 %collective-permute-start.1 = (bf16[48,768]{1,0:T(8,128)(2,1)S(1)}, bf16[48,768]{1,0:T(8,128)(2,1)S(1)}, u32[]{:S(2)}, u32[]{:S(2)}) collective-permute-start(bf16[48,768]{1,0:T(8,128)(2,1)S(1)} %get-tuple-element.10), channel_id=1, source_target_pairs={{0,248},{8,0},{16,8},{24,16},{32,24},{40,32},{48,40},{56,48},{64,5... | collective-permute-start | bytes 221192 | tf_op jit(solution)/shard_map/ppermute | solution.py:361
  71.3 0.0 collective-permute-start
  71.3 1.1 %fusion = (bf16[16,1,768]{2,1,0:T(2,128)(2,1)S(1)}, bf16[16,1,768]{2,1,0:T(2,128)(2,1)S(1)}) fusion(bf16[16,48,768]{2,1,0:T(8,128)(2,1)} %w_hbm.3), kind=kLoop, calls=%fused_computation.4 | loop fusion | bytes 98304 | tf_op jit(solution)/shard_map/slice | solution.py:396
  72.5 5.9 %collective-permute-start.2 = (bf16[16,768]{1,0:T(8,128)(2,1)S(1)}, bf16[16,768]{1,0:T(8,128)(2,1)S(1)}, u32[]{:S(2)}, u32[]{:S(2)}) collective-permute-start(bf16[16,768]{1,0:T(8,128)(2,1)S(1)} %bitcast.18), channel_id=1, source_target_pairs={{0,1},{1,2},{2,3},{3,4},{4,5},{5,6},{6,7},{7,0},{8,9},{9,10},{10,1... | collective-permute-start | bytes 73736 | tf_op jit(solution)/shard_map/ppermute | solution.py:361
  78.4 2.6 %collective-permute-start.3 = (bf16[16,768]{1,0:T(8,128)(2,1)S(1)}, bf16[16,768]{1,0:T(8,128)(2,1)S(1)}, u32[]{:S(2)}, u32[]{:S(2)}) collective-permute-start(bf16[16,768]{1,0:T(8,128)(2,1)S(1)} %bitcast.19), channel_id=1, source_target_pairs={{0,7},{1,0},{2,1},{3,2},{4,3},{5,4},{6,5},{7,6},{8,15},{9,8},{10,9... | collective-permute-start | bytes 73736 | tf_op jit(solution)/shard_map/ppermute | solution.py:361
  81.0 3.8 %collective-permute-done.2.wl = bf16[16,768]{1,0:T(8,128)(2,1)S(1)} collective-permute-done((bf16[16,768]{1,0:T(8,128)(2,1)S(1)}, bf16[16,768]{1,0:T(8,128)(2,1)S(1)}, u32[]{:S(2)}, u32[]{:S(2)}) %collective-permute-start.2) | collective-permute-done | bytes 24608 | tf_op jit(solution)/shard_map/ppermute | solution.py:361
  84.8 0.0 copy-start.4
  84.8 0.6 collective-permute-done.3.wh
  85.4 0.0 copy-start.5
  85.4 0.0 collective-permute-done.1.uh
  85.4 0.0 copy-start.2
  85.4 0.0 collective-permute-done.ul
  85.4 0.0 copy-start.3
  85.4 1.3 %all-to-all-done.1 = f32[256,3,1,128]{3,2,1,0:T(1,128)S(1)} async-done(((f32[256,3,1,128]{3,2,1,0:T(1,128)}), f32[256,3,1,128]{3,2,1,0:T(1,128)S(1)}, u32[]{:S(2)}, u32[]{:S(2)}) %all-to-all-start.1) | async-done | bytes 393248 | tf_op jit(solution)/shard_map/all_to_all | solution.py:445
  86.7 0.0 copy-start.1
  86.7 0.0 copy-done.4
  86.7 0.0 copy-done.5
  86.7 0.0 copy-done.2
  86.7 0.0 copy-done.3
  86.7 0.7 copy-done.1
  87.5 14.8 %backward.1 = (f32[16,48,768]{2,1,0:T(8,128)}, f32[16,48,768]{2,1,0:T(8,128)}, f32[16,48,768]{2,1,0:T(8,128)}, f32[16,48,768]{2,1,0:T(8,128)}) custom-call(bf16[16,48,768]{2,1,0:T(8,128)(2,1)} %u_hbm.3, bf16[16,48,768]{2,1,0:T(8,128)(2,1)} %v_hbm.3, bf16[16,48,768]{2,1,0:T(8,128)(2,1)} %w_hbm.3, bf16[48,768]{1,0:T(8,128)(2,1)} %copy-done.3, ...), custom_call_target="tpu_custom_call" | custom-call | flops 5888802816 | bytes 16766976 | tf_op jit(solution)/shard_map/backward/pallas_call | solution.py:367
  (2 shorter events, 0.0 us)
Async XLA Ops:
  18.5 34.2 %all-to-all-start = ((f32[256,3,1,128]{3,2,1,0:T(1,128)}), f32[256,3,1,128]{3,2,1,0:T(1,128)S(1)}, u32[]{:S(2)}, u32[]{:S(2)}) async-start(f32[256,3,1,128]{3,2,1,0:T(1,128)} %bitcast.17), calls=%async_computation | async-start | bytes 786432 | tf_op jit(solution)/shard_map/all_to_all | solution.py:426
  52.7 0.7 copy-start
  62.6 24.1 %all-to-all-start.1 = ((f32[256,3,1,128]{3,2,1,0:T(1,128)}), f32[256,3,1,128]{3,2,1,0:T(1,128)S(1)}, u32[]{:S(2)}, u32[]{:S(2)}) async-start(f32[256,3,1,128]{3,2,1,0:T(1,128)} %bitcast.14), calls=%async_computation.1 | async-start | bytes 786432 | tf_op jit(solution)/shard_map/all_to_all | solution.py:445
  69.0 16.4 %collective-permute-start.1 = (bf16[48,768]{1,0:T(8,128)(2,1)S(1)}, bf16[48,768]{1,0:T(8,128)(2,1)S(1)}, u32[]{:S(2)}, u32[]{:S(2)}) collective-permute-start(bf16[48,768]{1,0:T(8,128)(2,1)S(1)} %get-tuple-element.10), channel_id=1, source_target_pairs={{0,248},{8,0},{16,8},{24,16},{32,24},{40,32},{48,40},{56,48},{64,5... | collective-permute-start | bytes 221192 | tf_op jit(solution)/shard_map/ppermute | solution.py:361
  71.3 14.0 %collective-permute-start = (bf16[48,768]{1,0:T(8,128)(2,1)S(1)}, bf16[48,768]{1,0:T(8,128)(2,1)S(1)}, u32[]{:S(2)}, u32[]{:S(2)}) collective-permute-start(bf16[48,768]{1,0:T(8,128)(2,1)S(1)} %get-tuple-element.11), channel_id=1, source_target_pairs={{0,8},{8,16},{16,24},{24,32},{32,40},{40,48},{48,56},{56,64},{64,7... | collective-permute-start | bytes 221192 | tf_op jit(solution)/shard_map/ppermute | solution.py:361
  72.5 12.3 %collective-permute-start.2 = (bf16[16,768]{1,0:T(8,128)(2,1)S(1)}, bf16[16,768]{1,0:T(8,128)(2,1)S(1)}, u32[]{:S(2)}, u32[]{:S(2)}) collective-permute-start(bf16[16,768]{1,0:T(8,128)(2,1)S(1)} %bitcast.18), channel_id=1, source_target_pairs={{0,1},{1,2},{2,3},{3,4},{4,5},{5,6},{6,7},{7,0},{8,9},{9,10},{10,1... | collective-permute-start | bytes 73736 | tf_op jit(solution)/shard_map/ppermute | solution.py:361
  78.4 7.0 %collective-permute-start.3 = (bf16[16,768]{1,0:T(8,128)(2,1)S(1)}, bf16[16,768]{1,0:T(8,128)(2,1)S(1)}, u32[]{:S(2)}, u32[]{:S(2)}) collective-permute-start(bf16[16,768]{1,0:T(8,128)(2,1)S(1)} %bitcast.19), channel_id=1, source_target_pairs={{0,7},{1,0},{2,1},{3,2},{4,3},{5,4},{6,5},{7,6},{8,15},{9,8},{10,9... | collective-permute-start | bytes 73736 | tf_op jit(solution)/shard_map/ppermute | solution.py:361
  84.8 1.9 %copy-start.4 = (bf16[16,768]{1,0:T(8,128)(2,1)}, bf16[16,768]{1,0:T(8,128)(2,1)S(1)}, u32[]{:S(2)}) copy-start(bf16[16,768]{1,0:T(8,128)(2,1)S(1)} %collective-permute-done.2.wl) | copy-start | bytes 73732
  85.4 1.3 %copy-start.5 = (bf16[16,768]{1,0:T(8,128)(2,1)}, bf16[16,768]{1,0:T(8,128)(2,1)S(1)}, u32[]{:S(2)}) copy-start(bf16[16,768]{1,0:T(8,128)(2,1)S(1)} %collective-permute-done.3.wh) | copy-start | bytes 73732
  85.4 1.3 %copy-start.2 = (bf16[48,768]{1,0:T(8,128)(2,1)}, bf16[48,768]{1,0:T(8,128)(2,1)S(1)}, u32[]{:S(2)}) copy-start(bf16[48,768]{1,0:T(8,128)(2,1)S(1)} %collective-permute-done.1.uh) | copy-start | bytes 221188
  85.4 1.3 %copy-start.3 = (bf16[48,768]{1,0:T(8,128)(2,1)}, bf16[48,768]{1,0:T(8,128)(2,1)S(1)}, u32[]{:S(2)}) copy-start(bf16[48,768]{1,0:T(8,128)(2,1)S(1)} %collective-permute-done.ul) | copy-start | bytes 221188
  86.7 0.7 copy-start.1

commit v4 on v3

--- a/solution.py
+++ b/solution.py
@@ -193,7 +193,8 @@
 def owner_kernel(
     ngx, ngz, cx, cz, seen, hxh, hxl, hzh, hzl, lxh, lxl, lxth, lxtl, lzth, lztl, muz, mukx, mum, out
 ):
-    per = mum.shape[0]
+    per = mum.shape[0] // (ngx * ngz)
+    me = lax.axis_index("gx") * ngz + lax.axis_index("gz")
     nx, nz = ngx * cx, ngz * cz
     lane = lax.broadcasted_iota(jnp.int32, (ngx, LANES), 1)
     lane8 = lax.broadcasted_iota(jnp.int32, (ngz, LANES), 1)
@@ -228,7 +229,7 @@
         mine = f1[2 * ngx * m : 2 * ngx * (m + 1)]
         other = f2[2 * ngz * m : 2 * ngz * (m + 1)].T
         spec = dot3((lxh[...], lxl[...]), split(mine)) + dot3(split(other), (lzth[...], lztl[...]))
-        spec = spec / ((mukx[...] + muz[...] + mum[m : m + 1, :1]) * (-float(nx * nz)))
+        spec = spec / ((mukx[...] + muz[...] + mum[me * per + m]) * (-float(nx * nz)))
         spec = split(spec)
         ex.append(dot3((lxth[...], lxtl[...]), spec))
         ez.append(dot3((lzth[...], lztl[...]), spec, dot_t))
@@ -361,7 +362,7 @@
     return lax.ppermute(block, axis, [(i, (i + step) % count) for i in range(count)])
 
 
-def call(kernel, name, outs, scratch, flops, *args, places=(), out_places=()):
+def call(kernel, name, outs, scratch, flops, *args, places=(), out_places=(), vmem=60 << 20):
     spaces, out_spaces = dict(places), dict(out_places)
     size = sum(math.prod(a.shape) * a.dtype.itemsize for a in [*args, *outs])
     return pl.pallas_call(
@@ -374,7 +375,7 @@
             pl.BlockSpec(memory_space=out_spaces.get(i, pltpu.VMEM)) for i in range(len(outs))
         ],
         scratch_shapes=scratch,
-        compiler_params=pltpu.CompilerParams(vmem_limit_bytes=60 << 20),
+        compiler_params=pltpu.CompilerParams(vmem_limit_bytes=vmem),
         cost_estimate=pl.CostEstimate(flops=flops, bytes_accessed=size, transcendentals=0),
         name=name,
     )(*args)
@@ -389,7 +390,6 @@
     per = ny // devices
     cells = cx * cz
     edges = 2 * (cx + cz)
-    me = lax.axis_index("gx") * ngz + lax.axis_index("gz")
     u_low = shifted(u_vel[-1], "gx", 1)
     u_high = shifted(u_vel[0], "gx", -1)
     w_low = shifted(w_vel[:, -1], "gz", 1)
@@ -428,7 +428,6 @@
     block_x, block_z = np.arange(ngx) * cx, np.arange(ngz) * cz
     lx = hx[:, np.concatenate([(block_x - 1) % nx, (block_x + cx) % nx])]
     lz = hz[:, np.concatenate([(block_z - 1) % nz, (block_z + cz) % nz])]
-    lam_m = lax.dynamic_slice(jnp.asarray(mum[0]), (me * per,), (per,))
     (back,) = call(
         functools.partial(owner_kernel, ngx, ngz, cx, cz),
         "owner",
@@ -439,7 +438,9 @@
         *halves(hx), *halves(hz), *halves(lx), *halves(lx.T), *halves(lz.T),
         f32(periodic_eigen_np(nz).reshape(1, -1)),
         f32(periodic_eigen_np(nx).reshape(-1, 1)),
-        jnp.broadcast_to(lam_m[:, None], (per, LANES)),
+        f32(mum[0]),
+        places={13: pltpu.SMEM},
+        vmem=20 << 20,
     )
     back = back.reshape(devices, per, 1, edges)
     got = lax.all_to_all(back, ("gx", "gz"), split_axis=0, concat_axis=0, tiled=True)
@@ -463,6 +464,7 @@
             *tables, f32(to_cells), along_z, *halves(local.T), mux, mum,
             places={i: pl.ANY for i in (0, 1, 2, 8)},
             out_places={i: pl.ANY for i in range(4)},
+            vmem=60 << 20,
         )
     )
 

time: 103 us -> 101 us (0.981)
  blocking collectives: 0 us -> 34.2 us
  waiting for transfers between devices: 23.5 us -> 5.72 us
  starting transfers between devices: 31.9 us -> 16.3 us
  local copies, waits for them, and re-layouts: 4.3 us -> 2.89 us
  Pallas kernels: 41.8 us -> 40.7 us
    all_to_all x0 -> x1, blocking collectives: none -> 34.2 us  [on_device(): lax.all_to_all(send, ('gx', 'gz'), split_axis=0, concat_axis=0, tiled=True)]
    all_to_all x1 -> x0, waiting for transfers between devices: 17.7 us -> none  [on_device(): lax.all_to_all(send, ('gx', 'gz'), split_axis=0, concat_axis=0, tiled=True)]
    all_to_all x1 -> x0, starting transfers between devices: 15.7 us -> none  [on_device(): lax.all_to_all(send, ('gx', 'gz'), split_axis=0, concat_axis=0, tiled=True)]
    pallas_call x3, Pallas kernels: 41.8 us -> 40.7 us  [call(): pl.pallas_call(kernel, out_shape=outs, in_specs=[pl.BlockSpec(memory_spac...]
  transfers between devices with their start and end apart: 6 -> 5, of which waited for: 4 -> 3; matrix products, arithmetic and copies ran while one was open for 3% -> 2% of each run, Pallas kernels for 0% -> 0%
where the time goes in v4:
time: 101 us
  Pallas kernels  40.7 us (40%)
  blocking collectives  34.2 us (34%)
  starting transfers between devices  16.3 us (16%)
  waiting for transfers between devices  5.72 us (6%)
  local copies, waits for them, and re-layouts  2.89 us (3%)
  between operations  1.04 us (1%)
    pallas_call x3, Pallas kernels, call(): pl.pallas_call(kernel, out_shape=outs, in_specs=[pl.BlockSpec(memory_spac...  40.7 us
    all_to_all x1, blocking collectives, on_device(): lax.all_to_all(send, ('gx', 'gz'), split_axis=0, concat_axis=0, tiled=True)  34.2 us
    ppermute x4, starting transfers between devices, shifted(): lax.ppermute(block, axis, [(i, (i + step) % count) for i in range(count)])  10.9 us
    all_to_all x1, starting transfers between devices, on_device(): lax.all_to_all(back, ('gx', 'gz'), split_axis=0, concat_axis=0, tiled=True)  5.43 us
    ppermute x4, waiting for transfers between devices, shifted(): lax.ppermute(block, axis, [(i, (i + step) % count) for i in range(count)])  4.41 us
  transfers between devices with their start and end apart: 5, of which 3 were waited for; matrix products, arithmetic and copies ran while one was open for 2% of the time, Pallas kernels for 0%

profile of v4, /device:TPU:1, one launch (start us, length us, event | category | flops | bytes accessed | tf_op | source)
XLA Modules:
  0.0 100.8 jit_solution(16948044659552688995)
XLA Ops:
  0.6 0.0 copy-start
  0.6 0.0 copy-start.1
  0.7 0.0 copy-start.2
  0.7 0.0 copy-start.3
  0.7 0.0 copy-start.4
  0.7 0.0 copy-start.5
  0.7 0.0 copy-start.6
  0.7 0.0 copy-start.7
  0.7 0.0 copy-start.8
  0.7 0.0 copy-start.9
  0.8 0.0 copy-start.10
  0.8 0.0 copy-start.11
  0.8 0.0 copy-start.12
  0.8 18.1 %forward.1 = (f32[768,128]{1,0:T(8,128)}, f32[768,768]{1,0:T(8,128)}) custom-call(bf16[16,48,768]{2,1,0:T(8,128)(2,1)} %u_hbm.3, bf16[16,48,768]{2,1,0:T(8,128)(2,1)} %v_hbm.3, bf16[16,48,768]{2,1,0:T(8,128)(2,1)} %w_hbm.3, f32[24,768]{1,0:T(8,128)} %constant.52.clone.sa, f32[24,768]{1,0:T(8,128)} %constant.53.clone.ca, f32[32,768]{1,0:T(8,128)} %constant.54.clone.sb, ...), custom_call_target="tpu_custom_call" | custom-call | flops 5888802816 | bytes 7133184 | tf_op jit(solution)/shard_map/forward/pallas_call | solution.py:368
  18.9 34.2 %all_to_all.10 = f32[256,3,1,128]{3,2,1,0:T(1,128)S(1)} all-to-all(f32[256,3,1,128]{3,2,1,0:T(1,128)} %bitcast.16), channel_id=1, replica_groups=mesh['gx'=32,'gz'=8] {'gx','gz'}, dimensions={0} | all-to-all | bytes 786432 | tf_op jit(solution)/shard_map/all_to_all | solution.py:426
  53.1 0.0 copy-done.3
  53.1 0.0 copy-done.4
  53.2 7.8 %owner.1 = f32[768,128]{1,0:T(8,128)} custom-call(f32[768,128]{1,0:T(8,128)S(1)} %bitcast.14, bf16[512,512]{1,0:T(8,128)(2,1)S(1)} %copy-done.1, bf16[512,512]{1,0:T(8,128)(2,1)S(1)} %copy-done, bf16[384,384]{1,0:T(8,128)(2,1)S(1)} %copy-done.3, bf16[384,384]{1,0:T(8,128)(2,1)S(1)} %copy-done.2, bf16[512,64]{1,0:T(8,128)(2,1)S(1)} %copy-done.6, ...), custom_call_target="tpu_custom_call" | custom-call | flops 707788800 | bytes 2718208 | tf_op jit(solution)/shard_map/owner/pallas_call | solution.py:368
  61.0 5.4 %all-to-all-start.1 = ((f32[256,3,1,128]{3,2,1,0:T(1,128)}), f32[256,3,1,128]{3,2,1,0:T(1,128)S(1)}, u32[]{:S(2)}, u32[]{:S(2)}) async-start(f32[256,3,1,128]{3,2,1,0:T(1,128)} %bitcast.6), calls=%async_computation.1 | async-start | bytes 786432 | tf_op jit(solution)/shard_map/all_to_all | solution.py:446
  66.5 0.9 slice_bitcast_fusion
  67.4 2.4 %collective-permute-start.1 = (bf16[48,768]{1,0:T(8,128)(2,1)S(1)}, bf16[48,768]{1,0:T(8,128)(2,1)S(1)}, u32[]{:S(2)}, u32[]{:S(2)}) collective-permute-start(bf16[48,768]{1,0:T(8,128)(2,1)S(1)} %get-tuple-element.10), channel_id=1, source_target_pairs={{0,248},{8,0},{16,8},{24,16},{32,24},{40,32},{48,40},{56,48},{64,5... | collective-permute-start | bytes 221192 | tf_op jit(solution)/shard_map/ppermute | solution.py:362
  69.8 0.0 collective-permute-start
  69.8 1.1 %fusion = (bf16[16,1,768]{2,1,0:T(2,128)(2,1)S(1)}, bf16[16,1,768]{2,1,0:T(2,128)(2,1)S(1)}) fusion(bf16[16,48,768]{2,1,0:T(8,128)(2,1)} %w_hbm.3), kind=kLoop, calls=%fused_computation.4 | loop fusion | bytes 98304 | tf_op jit(solution)/shard_map/slice | solution.py:396
  70.9 5.9 %collective-permute-start.2 = (bf16[16,768]{1,0:T(8,128)(2,1)S(1)}, bf16[16,768]{1,0:T(8,128)(2,1)S(1)}, u32[]{:S(2)}, u32[]{:S(2)}) collective-permute-start(bf16[16,768]{1,0:T(8,128)(2,1)S(1)} %bitcast.17), channel_id=1, source_target_pairs={{0,1},{1,2},{2,3},{3,4},{4,5},{5,6},{6,7},{7,0},{8,9},{9,10},{10,1... | collective-permute-start | bytes 73736 | tf_op jit(solution)/shard_map/ppermute | solution.py:362
  76.8 2.6 %collective-permute-start.3 = (bf16[16,768]{1,0:T(8,128)(2,1)S(1)}, bf16[16,768]{1,0:T(8,128)(2,1)S(1)}, u32[]{:S(2)}, u32[]{:S(2)}) collective-permute-start(bf16[16,768]{1,0:T(8,128)(2,1)S(1)} %bitcast.18), channel_id=1, source_target_pairs={{0,7},{1,0},{2,1},{3,2},{4,3},{5,4},{6,5},{7,6},{8,15},{9,8},{10,9... | collective-permute-start | bytes 73736 | tf_op jit(solution)/shard_map/ppermute | solution.py:362
  79.4 3.8 %collective-permute-done.2.wl = bf16[16,768]{1,0:T(8,128)(2,1)S(1)} collective-permute-done((bf16[16,768]{1,0:T(8,128)(2,1)S(1)}, bf16[16,768]{1,0:T(8,128)(2,1)S(1)}, u32[]{:S(2)}, u32[]{:S(2)}) %collective-permute-start.2) | collective-permute-done | bytes 24608 | tf_op jit(solution)/shard_map/ppermute | solution.py:362
  83.2 0.6 collective-permute-done.3.wh
  83.8 0.0 collective-permute-done.1.uh
  83.8 0.0 collective-permute-done.ul
  83.8 1.3 %all-to-all-done.1 = f32[256,3,1,128]{3,2,1,0:T(1,128)S(1)} async-done(((f32[256,3,1,128]{3,2,1,0:T(1,128)}), f32[256,3,1,128]{3,2,1,0:T(1,128)S(1)}, u32[]{:S(2)}, u32[]{:S(2)}) %all-to-all-start.1) | async-done | bytes 393248 | tf_op jit(solution)/shard_map/all_to_all | solution.py:446
  85.1 0.7 copy-done.13
  85.9 14.8 %backward.1 = (f32[16,48,768]{2,1,0:T(8,128)}, f32[16,48,768]{2,1,0:T(8,128)}, f32[16,48,768]{2,1,0:T(8,128)}, f32[16,48,768]{2,1,0:T(8,128)}) custom-call(bf16[16,48,768]{2,1,0:T(8,128)(2,1)} %u_hbm.3, bf16[16,48,768]{2,1,0:T(8,128)(2,1)} %v_hbm.3, bf16[16,48,768]{2,1,0:T(8,128)(2,1)} %w_hbm.3, bf16[48,768]{1,0:T(8,128)(2,1)} %copy-done.15, ...), custom_call_target="tpu_custom_call" | custom-call | flops 5888802816 | bytes 16766976 | tf_op jit(solution)/shard_map/backward/pallas_call | solution.py:368
  (22 shorter events, 0.1 us)
Async XLA Ops:
  0.6 52.5 %copy-start = (bf16[512,512]{1,0:T(8,128)(2,1)S(1)}, bf16[512,512]{1,0:T(8,128)(2,1)}, u32[]{:S(2)}) copy-start(bf16[512,512]{1,0:T(8,128)(2,1)} %constant.63.clone.hxl) | copy-start | bytes 1572868
  0.6 52.4 %copy-start.1 = (bf16[512,512]{1,0:T(8,128)(2,1)S(1)}, bf16[512,512]{1,0:T(8,128)(2,1)}, u32[]{:S(2)}) copy-start(bf16[512,512]{1,0:T(8,128)(2,1)} %constant.62.clone.hxh) | copy-start | bytes 1572868
  0.7 52.4 %copy-start.2 = (bf16[384,384]{1,0:T(8,128)(2,1)S(1)}, bf16[384,384]{1,0:T(8,128)(2,1)}, u32[]{:S(2)}) copy-start(bf16[384,384]{1,0:T(8,128)(2,1)} %constant.65.clone.hzl) | copy-start | bytes 884740
  0.7 52.4 %copy-start.3 = (bf16[384,384]{1,0:T(8,128)(2,1)S(1)}, bf16[384,384]{1,0:T(8,128)(2,1)}, u32[]{:S(2)}) copy-start(bf16[384,384]{1,0:T(8,128)(2,1)} %constant.64.clone.hzh) | copy-start | bytes 884740
  0.7 52.4 %copy-start.4 = (f32[512,1]{1,0:T(8,128)S(1)}, f32[512,1]{1,0:T(8,128)}, u32[]{:S(2)}) copy-start(f32[512,1]{1,0:T(8,128)} %constant.73.clone.mukx) | copy-start | bytes 6148
  0.7 52.4 %copy-start.5 = (bf16[512,64]{1,0:T(8,128)(2,1)S(1)}, bf16[512,64]{1,0:T(8,128)(2,1)}, u32[]{:S(2)}) copy-start(bf16[512,64]{1,0:T(8,128)(2,1)} %constant.67.clone.lxl) | copy-start | bytes 196612
  0.7 52.4 %copy-start.6 = (bf16[512,64]{1,0:T(8,128)(2,1)S(1)}, bf16[512,64]{1,0:T(8,128)(2,1)}, u32[]{:S(2)}) copy-start(bf16[512,64]{1,0:T(8,128)(2,1)} %constant.66.clone.lxh) | copy-start | bytes 196612
  0.7 52.4 %copy-start.7 = (bf16[64,512]{1,0:T(8,128)(2,1)S(1)}, bf16[64,512]{1,0:T(8,128)(2,1)}, u32[]{:S(2)}) copy-start(bf16[64,512]{1,0:T(8,128)(2,1)} %constant.69.clone.lxtl) | copy-start | bytes 196612
  0.7 52.4 %copy-start.8 = (bf16[64,512]{1,0:T(8,128)(2,1)S(1)}, bf16[64,512]{1,0:T(8,128)(2,1)}, u32[]{:S(2)}) copy-start(bf16[64,512]{1,0:T(8,128)(2,1)} %constant.68.clone.lxth) | copy-start | bytes 196612
  0.7 52.4 %copy-start.9 = (bf16[16,384]{1,0:T(8,128)(2,1)S(1)}, bf16[16,384]{1,0:T(8,128)(2,1)}, u32[]{:S(2)}) copy-start(bf16[16,384]{1,0:T(8,128)(2,1)} %constant.71.clone.lztl) | copy-start | bytes 36868
  0.8 52.4 %copy-start.10 = (bf16[16,384]{1,0:T(8,128)(2,1)S(1)}, bf16[16,384]{1,0:T(8,128)(2,1)}, u32[]{:S(2)}) copy-start(bf16[16,384]{1,0:T(8,128)(2,1)} %constant.70.clone.lzth) | copy-start | bytes 36868
  0.8 52.4 %copy-start.11 = (f32[768]{0:T(1024)S(1)}, f32[768]{0:T(1024)}, u32[]{:S(2)}) copy-start(f32[768]{0:T(1024)} %constant.74.clone.mum) | copy-start | bytes 9220
  0.8 52.4 %copy-start.12 = (f32[1,384]{1,0:T(1,128)S(1)}, f32[1,384]{1,0:T(1,128)}, u32[]{:S(2)}) copy-start(f32[1,384]{1,0:T(1,128)} %constant.72.clone.muz) | copy-start | bytes 4612
  61.0 24.1 %all-to-all-start.1 = ((f32[256,3,1,128]{3,2,1,0:T(1,128)}), f32[256,3,1,128]{3,2,1,0:T(1,128)S(1)}, u32[]{:S(2)}, u32[]{:S(2)}) async-start(f32[256,3,1,128]{3,2,1,0:T(1,128)} %bitcast.6), calls=%async_computation.1 | async-start | bytes 786432 | tf_op jit(solution)/shard_map/all_to_all | solution.py:446
  67.4 16.4 %collective-permute-start.1 = (bf16[48,768]{1,0:T(8,128)(2,1)S(1)}, bf16[48,768]{1,0:T(8,128)(2,1)S(1)}, u32[]{:S(2)}, u32[]{:S(2)}) collective-permute-start(bf16[48,768]{1,0:T(8,128)(2,1)S(1)} %get-tuple-element.10), channel_id=1, source_target_pairs={{0,248},{8,0},{16,8},{24,16},{32,24},{40,32},{48,40},{56,48},{64,5... | collective-permute-start | bytes 221192 | tf_op jit(solution)/shard_map/ppermute | solution.py:362
  69.8 14.0 %collective-permute-start = (bf16[48,768]{1,0:T(8,128)(2,1)S(1)}, bf16[48,768]{1,0:T(8,128)(2,1)S(1)}, u32[]{:S(2)}, u32[]{:S(2)}) collective-permute-start(bf16[48,768]{1,0:T(8,128)(2,1)S(1)} %get-tuple-element.11), channel_id=1, source_target_pairs={{0,8},{8,16},{16,24},{24,32},{32,40},{40,48},{48,56},{56,64},{64,7... | collective-permute-start | bytes 221192 | tf_op jit(solution)/shard_map/ppermute | solution.py:362
  70.9 12.3 %collective-permute-start.2 = (bf16[16,768]{1,0:T(8,128)(2,1)S(1)}, bf16[16,768]{1,0:T(8,128)(2,1)S(1)}, u32[]{:S(2)}, u32[]{:S(2)}) collective-permute-start(bf16[16,768]{1,0:T(8,128)(2,1)S(1)} %bitcast.17), channel_id=1, source_target_pairs={{0,1},{1,2},{2,3},{3,4},{4,5},{5,6},{6,7},{7,0},{8,9},{9,10},{10,1... | collective-permute-start | bytes 73736 | tf_op jit(solution)/shard_map/ppermute | solution.py:362
  76.8 7.0 %collective-permute-start.3 = (bf16[16,768]{1,0:T(8,128)(2,1)S(1)}, bf16[16,768]{1,0:T(8,128)(2,1)S(1)}, u32[]{:S(2)}, u32[]{:S(2)}) collective-permute-start(bf16[16,768]{1,0:T(8,128)(2,1)S(1)} %bitcast.18), channel_id=1, source_target_pairs={{0,7},{1,0},{2,1},{3,2},{4,3},{5,4},{6,5},{7,6},{8,15},{9,8},{10,9... | collective-permute-start | bytes 73736 | tf_op jit(solution)/shard_map/ppermute | solution.py:362
  83.2 1.9 %copy-start.16 = (bf16[16,768]{1,0:T(8,128)(2,1)}, bf16[16,768]{1,0:T(8,128)(2,1)S(1)}, u32[]{:S(2)}) copy-start(bf16[16,768]{1,0:T(8,128)(2,1)S(1)} %collective-permute-done.2.wl) | copy-start | bytes 73732
  83.8 1.3 %copy-start.17 = (bf16[16,768]{1,0:T(8,128)(2,1)}, bf16[16,768]{1,0:T(8,128)(2,1)S(1)}, u32[]{:S(2)}) copy-start(bf16[16,768]{1,0:T(8,128)(2,1)S(1)} %collective-permute-done.3.wh) | copy-start | bytes 73732
  83.8 1.3 %copy-start.14 = (bf16[48,768]{1,0:T(8,128)(2,1)}, bf16[48,768]{1,0:T(8,128)(2,1)S(1)}, u32[]{:S(2)}) copy-start(bf16[48,768]{1,0:T(8,128)(2,1)S(1)} %collective-permute-done.1.uh) | copy-start | bytes 221188
  83.8 1.3 %copy-start.15 = (bf16[48,768]{1,0:T(8,128)(2,1)}, bf16[48,768]{1,0:T(8,128)(2,1)S(1)}, u32[]{:S(2)}) copy-start(bf16[48,768]{1,0:T(8,128)(2,1)S(1)} %collective-permute-done.ul) | copy-start | bytes 221188
  85.1 0.8 copy-start.13

commit v5 on v4

--- a/solution.py
+++ b/solution.py
@@ -424,6 +424,9 @@
     )
     send = send.reshape(devices, per, 1, edges)
     seen = lax.all_to_all(send, ("gx", "gz"), split_axis=0, concat_axis=0, tiled=True)
+    seen, u_low, u_high, w_low, w_high = lax.optimization_barrier(
+        (seen, u_low, u_high, w_low, w_high)
+    )
     hx, hz = hartley_np(nx), hartley_np(nz)
     block_x, block_z = np.arange(ngx) * cx, np.arange(ngz) * cz
     lx = hx[:, np.concatenate([(block_x - 1) % nx, (block_x + cx) % nx])]

time: 101 us -> 105 us (1.040)
  starting transfers between devices: 16.3 us -> 26.2 us
  blocking collectives: 34.2 us -> 29.4 us
    all_to_all x1, starting transfers between devices: 5.43 us -> 15.7 us  [on_device(): lax.all_to_all(send, ('gx', 'gz'), split_axis=0, concat_axis=0, tiled=True)]
    all_to_all x1, blocking collectives: 34.2 us -> 29.4 us  [on_device(): lax.all_to_all(back, ('gx', 'gz'), split_axis=0, concat_axis=0, tiled=True)]
where the time goes in v5:
time: 105 us
  Pallas kernels  39.9 us (38%)
  blocking collectives  29.4 us (28%)
  starting transfers between devices  26.2 us (25%)
  waiting for transfers between devices  5.9 us (6%)
  local copies, waits for them, and re-layouts  2.15 us (2%)
    pallas_call x3, Pallas kernels, call(): pl.pallas_call(kernel, out_shape=outs, in_specs=[pl.BlockSpec(memory_spac...  39.9 us
    all_to_all x1, blocking collectives, on_device(): lax.all_to_all(back, ('gx', 'gz'), split_axis=0, concat_axis=0, tiled=True)  29.4 us
    all_to_all x1, starting transfers between devices, on_device(): lax.all_to_all(send, ('gx', 'gz'), split_axis=0, concat_axis=0, tiled=True)  15.7 us
    ppermute x4, starting transfers between devices, shifted(): lax.ppermute(block, axis, [(i, (i + step) % count) for i in range(count)])  10.5 us
    ppermute x4, waiting for transfers between devices, shifted(): lax.ppermute(block, axis, [(i, (i + step) % count) for i in range(count)])  4.59 us
  transfers between devices with their start and end apart: 5, of which 3 were waited for; matrix products, arithmetic and copies ran while one was open for 2% of the time, Pallas kernels for 0%

profile of v5, /device:TPU:1, one launch (start us, length us, event | category | flops | bytes accessed | tf_op | source)
XLA Modules:
  0.0 104.6 jit_solution(7281289967627354607)
XLA Ops:
  0.6 0.0 copy-start
  0.6 0.0 copy-start.1
  0.7 0.0 copy-start.2
  0.7 0.0 copy-start.3
  0.7 0.0 copy-start.4
  0.7 0.0 copy-start.5
  0.7 0.0 copy-start.6
  0.7 0.0 copy-start.7
  0.7 0.0 copy-start.8
  0.7 0.0 copy-start.9
  0.8 0.0 copy-start.10
  0.8 0.0 copy-start.11
  0.8 0.0 copy-start.12
  0.8 18.0 %forward.1 = (f32[768,128]{1,0:T(8,128)}, f32[768,768]{1,0:T(8,128)}) custom-call(bf16[16,48,768]{2,1,0:T(8,128)(2,1)} %u_hbm.3, bf16[16,48,768]{2,1,0:T(8,128)(2,1)} %v_hbm.3, bf16[16,48,768]{2,1,0:T(8,128)(2,1)} %w_hbm.3, f32[24,768]{1,0:T(8,128)} %constant.52.clone.sa, f32[24,768]{1,0:T(8,128)} %constant.53.clone.ca, f32[32,768]{1,0:T(8,128)} %constant.54.clone.sb, ...), custom_call_target="tpu_custom_call" | custom-call | flops 5888802816 | bytes 7133184 | tf_op jit(solution)/shard_map/forward/pallas_call | solution.py:368
  18.8 15.7 %all-to-all-start = ((f32[256,3,1,128]{3,2,1,0:T(1,128)}), f32[256,3,1,128]{3,2,1,0:T(1,128)S(1)}, u32[]{:S(2)}, u32[]{:S(2)}) async-start(f32[256,3,1,128]{3,2,1,0:T(1,128)} %bitcast.16), calls=%async_computation | async-start | bytes 786432 | tf_op jit(solution)/shard_map/all_to_all | solution.py:426
  34.5 0.9 slice_bitcast_fusion
  35.4 2.2 %collective-permute-start.1 = (bf16[48,768]{1,0:T(8,128)(2,1)S(1)}, bf16[48,768]{1,0:T(8,128)(2,1)S(1)}, u32[]{:S(2)}, u32[]{:S(2)}) collective-permute-start(bf16[48,768]{1,0:T(8,128)(2,1)S(1)} %get-tuple-element.20), channel_id=1, source_target_pairs={{0,248},{8,0},{16,8},{24,16},{32,24},{40,32},{48,40},{56,48},{64,5... | collective-permute-start | bytes 221192 | tf_op jit(solution)/shard_map/ppermute | solution.py:362
  37.6 0.0 collective-permute-start
  37.6 1.1 %fusion = (bf16[16,1,768]{2,1,0:T(2,128)(2,1)S(1)}, bf16[16,1,768]{2,1,0:T(2,128)(2,1)S(1)}) fusion(bf16[16,48,768]{2,1,0:T(8,128)(2,1)} %w_hbm.3), kind=kLoop, calls=%fused_computation.4 | loop fusion | bytes 98304 | tf_op jit(solution)/shard_map/slice | solution.py:396
  38.8 5.9 %collective-permute-start.2 = (bf16[16,768]{1,0:T(8,128)(2,1)S(1)}, bf16[16,768]{1,0:T(8,128)(2,1)S(1)}, u32[]{:S(2)}, u32[]{:S(2)}) collective-permute-start(bf16[16,768]{1,0:T(8,128)(2,1)S(1)} %bitcast.18), channel_id=1, source_target_pairs={{0,1},{1,2},{2,3},{3,4},{4,5},{5,6},{6,7},{7,0},{8,9},{9,10},{10,1... | collective-permute-start | bytes 73736 | tf_op jit(solution)/shard_map/ppermute | solution.py:362
  44.7 2.4 %collective-permute-start.3 = (bf16[16,768]{1,0:T(8,128)(2,1)S(1)}, bf16[16,768]{1,0:T(8,128)(2,1)S(1)}, u32[]{:S(2)}, u32[]{:S(2)}) collective-permute-start(bf16[16,768]{1,0:T(8,128)(2,1)S(1)} %bitcast.19), channel_id=1, source_target_pairs={{0,7},{1,0},{2,1},{3,2},{4,3},{5,4},{6,5},{7,6},{8,15},{9,8},{10,9... | collective-permute-start | bytes 73736 | tf_op jit(solution)/shard_map/ppermute | solution.py:362
  47.1 4.0 %collective-permute-done.2.wl = bf16[16,768]{1,0:T(8,128)(2,1)S(1)} collective-permute-done((bf16[16,768]{1,0:T(8,128)(2,1)S(1)}, bf16[16,768]{1,0:T(8,128)(2,1)S(1)}, u32[]{:S(2)}, u32[]{:S(2)}) %collective-permute-start.2) | collective-permute-done | bytes 24608 | tf_op jit(solution)/shard_map/ppermute | solution.py:362
  51.1 0.6 collective-permute-done.3.wh
  51.7 0.0 collective-permute-done.1.uh
  51.7 0.0 collective-permute-done.ul
  51.7 1.3 %all-to-all-done = f32[256,3,1,128]{3,2,1,0:T(1,128)S(1)} async-done(((f32[256,3,1,128]{3,2,1,0:T(1,128)}), f32[256,3,1,128]{3,2,1,0:T(1,128)S(1)}, u32[]{:S(2)}, u32[]{:S(2)}) %all-to-all-start) | async-done | bytes 393248 | tf_op jit(solution)/shard_map/all_to_all | solution.py:426
  53.0 0.0 copy-done.3
  53.0 0.0 copy-done.4
  53.0 0.0 copy-done.5
  53.1 7.1 %owner.1 = f32[768,128]{1,0:T(8,128)S(1)} custom-call(f32[768,128]{1,0:T(8,128)S(1)} %bitcast.14, bf16[512,512]{1,0:T(8,128)(2,1)S(1)} %copy-done.1, bf16[512,512]{1,0:T(8,128)(2,1)S(1)} %copy-done, bf16[384,384]{1,0:T(8,128)(2,1)S(1)} %copy-done.3, bf16[384,384]{1,0:T(8,128)(2,1)S(1)} %copy-done.2, bf16[512,64]{1,0:T(8,128)(2,1)S(1)} %copy-done.6, ...), custom_call_target="tpu_custom_call" | custom-call | flops 707788800 | bytes 2718208 | tf_op jit(solution)/shard_map/owner/pallas_call | solution.py:368
  60.2 29.4 %all_to_all.10 = f32[256,3,1,128]{3,2,1,0:T(1,128)} all-to-all(f32[256,3,1,128]{3,2,1,0:T(1,128)S(1)} %bitcast.15), channel_id=1, replica_groups=mesh['gx'=32,'gz'=8] {'gx','gz'}, dimensions={0} | all-to-all | bytes 786432 | tf_op jit(solution)/shard_map/all_to_all | solution.py:449
  89.6 14.8 %backward.1 = (f32[16,48,768]{2,1,0:T(8,128)}, f32[16,48,768]{2,1,0:T(8,128)}, f32[16,48,768]{2,1,0:T(8,128)}, f32[16,48,768]{2,1,0:T(8,128)}) custom-call(bf16[16,48,768]{2,1,0:T(8,128)(2,1)} %u_hbm.3, bf16[16,48,768]{2,1,0:T(8,128)(2,1)} %v_hbm.3, bf16[16,48,768]{2,1,0:T(8,128)(2,1)} %w_hbm.3, bf16[48,768]{1,0:T(8,128)(2,1)} %copy-done.14, ...), custom_call_target="tpu_custom_call" | custom-call | flops 5888802816 | bytes 16766976 | tf_op jit(solution)/shard_map/backward/pallas_call | solution.py:368
  (20 shorter events, 0.0 us)
Async XLA Ops:
  0.6 52.4 %copy-start = (bf16[512,512]{1,0:T(8,128)(2,1)S(1)}, bf16[512,512]{1,0:T(8,128)(2,1)}, u32[]{:S(2)}) copy-start(bf16[512,512]{1,0:T(8,128)(2,1)} %constant.63.clone.hxl) | copy-start | bytes 1572868
  0.6 52.4 %copy-start.1 = (bf16[512,512]{1,0:T(8,128)(2,1)S(1)}, bf16[512,512]{1,0:T(8,128)(2,1)}, u32[]{:S(2)}) copy-start(bf16[512,512]{1,0:T(8,128)(2,1)} %constant.62.clone.hxh) | copy-start | bytes 1572868
  0.7 52.3 %copy-start.2 = (bf16[384,384]{1,0:T(8,128)(2,1)S(1)}, bf16[384,384]{1,0:T(8,128)(2,1)}, u32[]{:S(2)}) copy-start(bf16[384,384]{1,0:T(8,128)(2,1)} %constant.65.clone.hzl) | copy-start | bytes 884740
  0.7 52.3 %copy-start.3 = (bf16[384,384]{1,0:T(8,128)(2,1)S(1)}, bf16[384,384]{1,0:T(8,128)(2,1)}, u32[]{:S(2)}) copy-start(bf16[384,384]{1,0:T(8,128)(2,1)} %constant.64.clone.hzh) | copy-start | bytes 884740
  0.7 52.3 %copy-start.4 = (f32[512,1]{1,0:T(8,128)S(1)}, f32[512,1]{1,0:T(8,128)}, u32[]{:S(2)}) copy-start(f32[512,1]{1,0:T(8,128)} %constant.73.clone.mukx) | copy-start | bytes 6148
  0.7 52.3 %copy-start.5 = (bf16[512,64]{1,0:T(8,128)(2,1)S(1)}, bf16[512,64]{1,0:T(8,128)(2,1)}, u32[]{:S(2)}) copy-start(bf16[512,64]{1,0:T(8,128)(2,1)} %constant.67.clone.lxl) | copy-start | bytes 196612
  0.7 52.3 %copy-start.6 = (bf16[512,64]{1,0:T(8,128)(2,1)S(1)}, bf16[512,64]{1,0:T(8,128)(2,1)}, u32[]{:S(2)}) copy-start(bf16[512,64]{1,0:T(8,128)(2,1)} %constant.66.clone.lxh) | copy-start | bytes 196612
  0.7 52.3 %copy-start.7 = (bf16[64,512]{1,0:T(8,128)(2,1)S(1)}, bf16[64,512]{1,0:T(8,128)(2,1)}, u32[]{:S(2)}) copy-start(bf16[64,512]{1,0:T(8,128)(2,1)} %constant.69.clone.lxtl) | copy-start | bytes 196612
  0.7 52.3 %copy-start.8 = (bf16[64,512]{1,0:T(8,128)(2,1)S(1)}, bf16[64,512]{1,0:T(8,128)(2,1)}, u32[]{:S(2)}) copy-start(bf16[64,512]{1,0:T(8,128)(2,1)} %constant.68.clone.lxth) | copy-start | bytes 196612
  0.7 52.3 %copy-start.9 = (bf16[16,384]{1,0:T(8,128)(2,1)S(1)}, bf16[16,384]{1,0:T(8,128)(2,1)}, u32[]{:S(2)}) copy-start(bf16[16,384]{1,0:T(8,128)(2,1)} %constant.71.clone.lztl) | copy-start | bytes 36868
  0.8 52.3 %copy-start.10 = (bf16[16,384]{1,0:T(8,128)(2,1)S(1)}, bf16[16,384]{1,0:T(8,128)(2,1)}, u32[]{:S(2)}) copy-start(bf16[16,384]{1,0:T(8,128)(2,1)} %constant.70.clone.lzth) | copy-start | bytes 36868
  0.8 52.3 %copy-start.11 = (f32[768]{0:T(1024)S(1)}, f32[768]{0:T(1024)}, u32[]{:S(2)}) copy-start(f32[768]{0:T(1024)} %constant.74.clone.mum) | copy-start | bytes 9220
  0.8 52.3 %copy-start.12 = (f32[1,384]{1,0:T(1,128)S(1)}, f32[1,384]{1,0:T(1,128)}, u32[]{:S(2)}) copy-start(f32[1,384]{1,0:T(1,128)} %constant.72.clone.muz) | copy-start | bytes 4612
  18.8 34.2 %all-to-all-start = ((f32[256,3,1,128]{3,2,1,0:T(1,128)}), f32[256,3,1,128]{3,2,1,0:T(1,128)S(1)}, u32[]{:S(2)}, u32[]{:S(2)}) async-start(f32[256,3,1,128]{3,2,1,0:T(1,128)} %bitcast.16), calls=%async_computation | async-start | bytes 786432 | tf_op jit(solution)/shard_map/all_to_all | solution.py:426
  35.4 16.2 %collective-permute-start.1 = (bf16[48,768]{1,0:T(8,128)(2,1)S(1)}, bf16[48,768]{1,0:T(8,128)(2,1)S(1)}, u32[]{:S(2)}, u32[]{:S(2)}) collective-permute-start(bf16[48,768]{1,0:T(8,128)(2,1)S(1)} %get-tuple-element.20), channel_id=1, source_target_pairs={{0,248},{8,0},{16,8},{24,16},{32,24},{40,32},{48,40},{56,48},{64,5... | collective-permute-start | bytes 221192 | tf_op jit(solution)/shard_map/ppermute | solution.py:362
  37.6 14.0 %collective-permute-start = (bf16[48,768]{1,0:T(8,128)(2,1)S(1)}, bf16[48,768]{1,0:T(8,128)(2,1)S(1)}, u32[]{:S(2)}, u32[]{:S(2)}) collective-permute-start(bf16[48,768]{1,0:T(8,128)(2,1)S(1)} %get-tuple-element.21), channel_id=1, source_target_pairs={{0,8},{8,16},{16,24},{24,32},{32,40},{40,48},{48,56},{56,64},{64,7... | collective-permute-start | bytes 221192 | tf_op jit(solution)/shard_map/ppermute | solution.py:362
  38.8 12.3 %collective-permute-start.2 = (bf16[16,768]{1,0:T(8,128)(2,1)S(1)}, bf16[16,768]{1,0:T(8,128)(2,1)S(1)}, u32[]{:S(2)}, u32[]{:S(2)}) collective-permute-start(bf16[16,768]{1,0:T(8,128)(2,1)S(1)} %bitcast.18), channel_id=1, source_target_pairs={{0,1},{1,2},{2,3},{3,4},{4,5},{5,6},{6,7},{7,0},{8,9},{9,10},{10,1... | collective-permute-start | bytes 73736 | tf_op jit(solution)/shard_map/ppermute | solution.py:362
  44.7 7.0 %collective-permute-start.3 = (bf16[16,768]{1,0:T(8,128)(2,1)S(1)}, bf16[16,768]{1,0:T(8,128)(2,1)S(1)}, u32[]{:S(2)}, u32[]{:S(2)}) collective-permute-start(bf16[16,768]{1,0:T(8,128)(2,1)S(1)} %bitcast.19), channel_id=1, source_target_pairs={{0,7},{1,0},{2,1},{3,2},{4,3},{5,4},{6,5},{7,6},{8,15},{9,8},{10,9... | collective-permute-start | bytes 73736 | tf_op jit(solution)/shard_map/ppermute | solution.py:362
  51.1 38.5 %copy-start.15 = (bf16[16,768]{1,0:T(8,128)(2,1)}, bf16[16,768]{1,0:T(8,128)(2,1)S(1)}, u32[]{:S(2)}) copy-start(bf16[16,768]{1,0:T(8,128)(2,1)S(1)} %collective-permute-done.2.wl) | copy-start | bytes 73732
  51.7 37.9 %copy-start.16 = (bf16[16,768]{1,0:T(8,128)(2,1)}, bf16[16,768]{1,0:T(8,128)(2,1)S(1)}, u32[]{:S(2)}) copy-start(bf16[16,768]{1,0:T(8,128)(2,1)S(1)} %collective-permute-done.3.wh) | copy-start | bytes 73732
  51.7 37.9 %copy-start.13 = (bf16[48,768]{1,0:T(8,128)(2,1)}, bf16[48,768]{1,0:T(8,128)(2,1)S(1)}, u32[]{:S(2)}) copy-start(bf16[48,768]{1,0:T(8,128)(2,1)S(1)} %collective-permute-done.1.uh) | copy-start | bytes 221188
  51.7 37.9 %copy-start.14 = (bf16[48,768]{1,0:T(8,128)(2,1)}, bf16[48,768]{1,0:T(8,128)(2,1)S(1)}, u32[]{:S(2)}) copy-start(bf16[48,768]{1,0:T(8,128)(2,1)S(1)} %collective-permute-done.ul) | copy-start | bytes 221188
